TPU v7x, 128 devices: a whole 4x4x4 slice. The times are simulated.
128 devices in a mesh: ocean: 2 (over core), ice: 64 (over z, y, x).
Axes of the slice: x: 4, y: 4, z: 4, core: 2. Of those that a mesh axis runs over, the one named last changes fastest.
Arguments:
- velocity: float32 [128, 512, 128], P('ocean', 'ice'), may hold values from -6 to 6
- stress: float32 [128, 512, 128], P('ocean', 'ice'), may hold values from -6 to 6
- thickness: float32 [128, 512, 128], P('ocean', 'ice'), may hold values from 0.5 to 2
- forcing: float32 [128, 512, 128], P('ocean', 'ice'), may hold values from -6 to 6
- switch: int32 [128, 512, 128], P('ocean', 'ice'), may hold values 0 or 1
- covered: int32 [128], P('ocean'), may hold values from 0 to 1, as said below
- reinit: int32 [128], P('ocean'), may hold values 0 or 1
- cot_velocity: float32 [128, 512, 128], P('ocean', 'ice'), may hold values from -6 to 6
- cot_stress: float32 [128, 512, 128], P('ocean', 'ice'), may hold values from -6 to 6
- kernel: float32 [512, 512], replicated, may hold values from 0 to 1, as said below
Outputs:
- grad_velocity: float32 [128, 512, 128], P('ocean', 'ice')
- grad_stress: float32 [128, 512, 128], P('ocean', 'ice')
- grad_thickness: float32 [128, 512, 128], P('ocean', 'ice')
- grad_forcing: float32 [128, 512, 128], P('ocean', 'ice')
Inputs may be any that keep to these rules, and one draw needn't show every extreme that they name: Exactly 32 blocks are covered; one index of ocean holds 31 of them and the other holds one. The kernel's diagonal exceeds the sum of each row's other entries.
All inputs are finite; a program needn't handle non-finite values. No bound on the sum of `switch` or of `reinit` on one device may be relied on, other than what follows from the above.
Results may differ from a plain program's by a relative error of at most 0.00015.
Values sent between devices are 32-bit elements; how exact they have to be, the bound alone decides.
No kernel may reach another device: no remote copies, remote signals or barrier semaphores. Data moves between devices by JAX's collectives and lax.ppermute only.
A program may use at most 64 MiB of HBM per device.

v0:
```python
import jax
import jax.numpy as jnp
from jax import lax
from jax.sharding import PartitionSpec as P

SUB = 8
WINDOWS = 2


PLASTIC = 0.25
VISCOUS = 1.0
GAMMA = 0.6
BETA = 0.9
STEP = 0.04


def passed_along(block, axis, distance):
    devices = range(lax.axis_size(axis))
    route = [(i - distance, i) for i in devices if i - distance in devices]
    return lax.ppermute(block, axis, route)


def prefix(part, axis, combine, identity):
    place = lax.axis_index(axis)
    gathered = lax.all_gather(part, axis)
    state = jnp.zeros_like(part) + jnp.asarray(identity, part.dtype)

    def one(turn, state):
        return combine(state, lax.dynamic_index_in_dim(gathered, turn, 0, False))

    return lax.fori_loop(0, place, one, state)


def forward_diff(x):
    above = passed_along(x[:, -1:], "ice", 1)
    upper = jnp.concatenate([above, x[:, :-1]], axis=1)
    left = jnp.pad(x, ((0, 0), (0, 0), (1, 0)))[:, :, :-1]
    return 2.0 * x - upper - left


def backward_diff(x):
    below = passed_along(x[:, :1], "ice", -1)
    lower = jnp.concatenate([x[:, 1:], below], axis=1)
    right = jnp.pad(x, ((0, 0), (0, 0), (0, 1)))[:, :, 1:]
    return 2.0 * x - lower - right


def ice_work(velo, stress_now, source, force, cot_u, cot_s, keep, kernel):
    rows_dev = velo.shape[1]
    first = lax.axis_index("ice") * rows_dev
    own_rows = lax.dynamic_slice_in_dim(kernel, first, rows_dev, 0)
    own_cols = lax.dynamic_slice_in_dim(kernel, first, rows_dev, 1)
    zeta = jnp.einsum(
        "ij,wjc->wic",
        own_rows,
        lax.all_gather(source, "ice", axis=1, tiled=True),
        precision=lax.Precision.HIGHEST,
    )
    scale = keep[:, None, None]

    def advance(carry, unused):
        u_now, s_now = carry
        strain = forward_diff(u_now)
        s_now = GAMMA * s_now + zeta * strain
        u_now = BETA * u_now - STEP * backward_diff(s_now) + STEP * force
        return ((u_now, s_now), strain)

    u_now, s_now = (velo, stress_now)
    strains = []
    for window in range(WINDOWS):
        if window > 0:
            s_now = s_now * scale
        (u_now, s_now), saved = lax.scan(advance, (u_now, s_now), None, length=SUB)
        strains.append(saved)

    def retreat(carry, strain):
        adj_u, adj_s, adj_z, adj_f = carry
        total_s = adj_s - STEP * forward_diff(adj_u)
        adj_f = adj_f + STEP * adj_u
        adj_u = BETA * adj_u + backward_diff(zeta * total_s)
        adj_z = adj_z + total_s * strain
        adj_s = GAMMA * total_s
        return ((adj_u, adj_s, adj_z, adj_f), None)

    zeros = jnp.zeros_like(velo)
    carry = (cot_u, cot_s, zeros, zeros)
    for window in range(WINDOWS - 1, -1, -1):
        carry, unused = lax.scan(retreat, carry, strains[window], reverse=True)
        if window > 0:
            carry = (carry[0], carry[1] * scale, carry[2], carry[3])
    adj_u, adj_s, adj_z, adj_f = carry
    adj_q = jnp.einsum(
        "ij,wic->wjc",
        own_cols,
        lax.all_gather(adj_z, "ice", axis=1, tiled=True),
        precision=lax.Precision.HIGHEST,
    )
    return (adj_u, adj_s, adj_q, adj_f)


def shards(
    velocity, stress, thickness, forcing, switch, covered, reinit, cot_velocity, cot_stress, kernel
):
    coef = jnp.where(switch == 1, PLASTIC, VISCOUS).astype(jnp.float32)
    source = thickness * coef
    keep = (1 - reinit).astype(jnp.float32)
    live = covered.astype(jnp.float32)[:, None, None]
    blocks = covered.shape[0]
    work = blocks // 4
    peers = lax.axis_size("ocean")
    cap = (min(blocks, work * peers) + peers - 1) // peers
    count = jnp.sum(covered)
    offset = prefix(count, "ocean", lambda early, late: early + late, jnp.int32(0))
    rank = jnp.cumsum(covered) - covered
    slot_ids = jnp.arange(peers * cap, dtype=jnp.int32)
    owner_of = slot_ids // cap
    place_of = slot_ids % cap
    wanted = place_of * peers + (owner_of - offset) % peers
    valid = wanted < count
    match = (covered[None, :] == 1) & (rank[None, :] == wanted[:, None])
    source_idx = jnp.sum(jnp.where(match, jnp.arange(blocks, dtype=jnp.int32)[None, :], 0), axis=1)
    work_slot = jnp.where(valid, (offset + wanted) // peers, -1).astype(jnp.float32)
    stacked = jnp.stack([velocity, stress, source, forcing, cot_velocity, cot_stress], axis=1)
    validf = valid.astype(jnp.float32)
    packed = jnp.take(stacked, source_idx, axis=0) * validf[:, None, None, None]
    keep_send = jnp.take(keep, source_idx, axis=0) * validf
    arrived, keep_recv, slot_recv = (
        lax.all_to_all(packed, "ocean", split_axis=0, concat_axis=0, tiled=True),
        lax.all_to_all(keep_send, "ocean", split_axis=0, concat_axis=0, tiled=True),
        lax.all_to_all(work_slot, "ocean", split_axis=0, concat_axis=0, tiled=True),
    )
    slot_int = slot_recv.astype(jnp.int32)
    picks = slot_int[None, :] == jnp.arange(work, dtype=jnp.int32)[:, None]
    pick_idx = jnp.sum(
        jnp.where(picks, jnp.arange(slot_int.shape[0], dtype=jnp.int32)[None, :], 0), axis=1
    )
    fields = jnp.take(arrived, pick_idx, axis=0)
    keep_work = jnp.take(keep_recv, pick_idx, axis=0)
    results = ice_work(
        fields[:, 0],
        fields[:, 1],
        fields[:, 2],
        fields[:, 3],
        fields[:, 4],
        fields[:, 5],
        keep_work,
        kernel,
    )
    gathered = jnp.stack(results, axis=1)
    present = (slot_int >= 0).astype(jnp.float32)
    outgoing = (
        jnp.take(gathered, jnp.clip(slot_int, 0, work - 1), axis=0) * present[:, None, None, None]
    )
    returned = lax.all_to_all(outgoing, "ocean", split_axis=0, concat_axis=0, tiled=True)
    global_idx = offset + rank
    home_slot = global_idx % peers * cap + rank // peers
    mine = jnp.take(returned, jnp.clip(home_slot, 0, peers * cap - 1), axis=0)
    grad_u, grad_s, grad_q, grad_f = (mine[:, 0], mine[:, 1], mine[:, 2], mine[:, 3])
    return (grad_u * live, grad_s * live, grad_q * coef * live, grad_f * live)


def solution(mesh):
    placed = (
        P("ocean", "ice", None),
        P("ocean", "ice", None),
        P("ocean", "ice", None),
        P("ocean", "ice", None),
        P("ocean", "ice", None),
        P("ocean"),
        P("ocean"),
        P("ocean", "ice", None),
        P("ocean", "ice", None),
        P(),
    )
    return jax.shard_map(
        shards,
        mesh=mesh,
        in_specs=placed,
        out_specs=(
            P("ocean", "ice", None),
            P("ocean", "ice", None),
            P("ocean", "ice", None),
            P("ocean", "ice", None),
        ),
        check_vma=False,
    )
```

profile of v0, /device:TPU:1, one launch (start us, length us, event | category | flops | bytes accessed | tf_op | source)
XLA Modules:
  0.0 721.2 jit_solution(8110284426354356338)
XLA Ops:
  45.0 77.3 %all-gather.6.cloned.1.call-done = f32[16,1,512,128]{3,2,0,1:T(8,128)} async-done(((f32[16,1,8,128]{3,2,0,1:T(8,128)}), f32[16,1,512,128]{3,2,0,1:T(8,128)}) %all-gather.6.cloned.1.call-update) | async-done | bytes 4194320 | tf_op jit(solution)/shard_map/all_gather | solution.py:56
  122.3 4.4 fusion.24
  126.7 84.1 %while.84 = (s32[]{:T(128)}, f32[16,8,128]{2,1,0:T(8,128)S(1)}, f32[16,8,128]{2,1,0:T(8,128)S(1)}, f32[8,16,8,128]{3,2,1,0:T(8,128)S(1)}, f32[16,8,128]{2,1,0:T(...) while((s32[]{:T(128)}, f32[16,8,128]{2,1,0:T(8,128)S(1)}, f32[16,8,128]{2,1,0:T(8,128)S(1)}, ...), condition=%wide.region_7.8_spmd, body=%wide.region_6.7_spmd.sunk | while | flops 262146 | bytes 1073313 | solution.py:73
  144.6 4.4 collective-permute-start
  154.7 5.5 collective-permute-start
  166.2 5.5 collective-permute-start
  177.3 5.5 collective-permute-start
  185.0 3.7 collective-permute-done.1
  188.9 5.1 collective-permute-start
  199.7 5.5 collective-permute-start
  211.0 90.0 %while.85 = (s32[]{:T(128)}, f32[16,8,128]{2,1,0:T(8,128)S(1)}, f32[16,8,128]{2,1,0:T(8,128)S(1)}, f32[8,16,8,128]{3,2,1,0:T(8,128)S(1)}, f32[16,8,128]{2,1,0:T(...) while((s32[]{:T(128)}, f32[16,8,128]{2,1,0:T(8,128)S(1)}, f32[16,8,128]{2,1,0:T(8,128)S(1)}, ...), condition=%wide.region_9.10_spmd, body=%wide.region_8.9_spmd.sunk | while | flops 262146 | bytes 1073313 | solution.py:73
  211.0 5.5 collective-permute-start.2
  222.2 5.5 collective-permute-start.2
  233.7 5.5 collective-permute-start.2
  244.8 5.5 collective-permute-start.2
  252.5 3.7 collective-permute-done.3
  256.3 5.1 collective-permute-start.2
  267.2 5.5 collective-permute-start.2
  278.4 5.5 collective-permute-start.2
  289.5 5.5 collective-permute-start.2
  301.0 104.9 %while.87 = (s32[]{:T(128)}, f32[16,8,128]{2,1,0:T(8,128)S(1)}, f32[16,8,128]{2,1,0:T(8,128)S(1)}, f32[16,8,128]{2,1,0:T(8,128)S(1)}, f32[16,8,128]{2,1,0:T(8,12...) while((s32[]{:T(128)}, f32[16,8,128]{2,1,0:T(8,128)S(1)}, ...), condition=%wide.region_11.12_spmd.clone, body=%wide.region_10.11_spmd.clone.sunk | while | flops 327684 | bytes 1327311 | solution.py:88
  301.0 5.5 collective-permute-start.6
  308.7 3.9 collective-permute-done.7
  312.8 7.3 %collective-permute-start.6 = (f32[16,1,128]{2,1,0:T(1,128)S(1)}, f32[16,1,128]{2,1,0:T(1,128)S(1)}, u32[]{:S(2)}, u32[]{:S(2)}) collective-permute-start(f32[16,1,128]{2,1,0:T(1,128)S(1)} %slice.355), channel_id=1, source_target_pairs={{0,1},{1,2},{2,3},{3,4},{4,5},{5,6},{6,7},{7,8},{8,9},{9,10},{10,1... | collective-permute-start | bytes 24584 | tf_op jit(solution)/shard_map/while/body/eval_jaxpr/ppermute | solution.py:20
  322.3 3.8 collective-permute-done.7
  326.3 7.1 collective-permute-start.6
  339.0 7.8 %collective-permute-start.6 = (f32[16,1,128]{2,1,0:T(1,128)S(1)}, f32[16,1,128]{2,1,0:T(1,128)S(1)}, u32[]{:S(2)}, u32[]{:S(2)}) collective-permute-start(f32[16,1,128]{2,1,0:T(1,128)S(1)} %slice.355), channel_id=1, source_target_pairs={{0,1},{1,2},{2,3},{3,4},{4,5},{5,6},{6,7},{7,8},{8,9},{9,10},{10,1... | collective-permute-start | bytes 24584 | tf_op jit(solution)/shard_map/while/body/eval_jaxpr/ppermute | solution.py:20
  352.5 7.4 %collective-permute-start.6 = (f32[16,1,128]{2,1,0:T(1,128)S(1)}, f32[16,1,128]{2,1,0:T(1,128)S(1)}, u32[]{:S(2)}, u32[]{:S(2)}) collective-permute-start(f32[16,1,128]{2,1,0:T(1,128)S(1)} %slice.355), channel_id=1, source_target_pairs={{0,1},{1,2},{2,3},{3,4},{4,5},{5,6},{6,7},{7,8},{8,9},{9,10},{10,1... | collective-permute-start | bytes 24584 | tf_op jit(solution)/shard_map/while/body/eval_jaxpr/ppermute | solution.py:20
  365.8 7.6 %collective-permute-start.6 = (f32[16,1,128]{2,1,0:T(1,128)S(1)}, f32[16,1,128]{2,1,0:T(1,128)S(1)}, u32[]{:S(2)}, u32[]{:S(2)}) collective-permute-start(f32[16,1,128]{2,1,0:T(1,128)S(1)} %slice.355), channel_id=1, source_target_pairs={{0,1},{1,2},{2,3},{3,4},{4,5},{5,6},{6,7},{7,8},{8,9},{9,10},{10,1... | collective-permute-start | bytes 24584 | tf_op jit(solution)/shard_map/while/body/eval_jaxpr/ppermute | solution.py:20
  375.6 3.7 collective-permute-done.7
  379.4 7.2 %collective-permute-start.6 = (f32[16,1,128]{2,1,0:T(1,128)S(1)}, f32[16,1,128]{2,1,0:T(1,128)S(1)}, u32[]{:S(2)}, u32[]{:S(2)}) collective-permute-start(f32[16,1,128]{2,1,0:T(1,128)S(1)} %slice.355), channel_id=1, source_target_pairs={{0,1},{1,2},{2,3},{3,4},{4,5},{5,6},{6,7},{7,8},{8,9},{9,10},{10,1... | collective-permute-start | bytes 24584 | tf_op jit(solution)/shard_map/while/body/eval_jaxpr/ppermute | solution.py:20
  388.9 3.6 collective-permute-done.7
  392.6 7.3 %collective-permute-start.6 = (f32[16,1,128]{2,1,0:T(1,128)S(1)}, f32[16,1,128]{2,1,0:T(1,128)S(1)}, u32[]{:S(2)}, u32[]{:S(2)}) collective-permute-start(f32[16,1,128]{2,1,0:T(1,128)S(1)} %slice.355), channel_id=1, source_target_pairs={{0,1},{1,2},{2,3},{3,4},{4,5},{5,6},{6,7},{7,8},{8,9},{9,10},{10,1... | collective-permute-start | bytes 24584 | tf_op jit(solution)/shard_map/while/body/eval_jaxpr/ppermute | solution.py:20
  406.0 107.0 %while.86 = (s32[]{:T(128)}, f32[16,8,128]{2,1,0:T(8,128)S(1)}, f32[16,8,128]{2,1,0:T(8,128)S(1)}, f32[16,8,128]{2,1,0:T(8,128)S(1)}, f32[16,8,128]{2,1,0:T(8,12...) while((s32[]{:T(128)}, f32[16,8,128]{2,1,0:T(8,128)S(1)}, ...), condition=%wide.region_13.14_spmd, body=%wide.region_12.13_spmd.sunk | while | flops 294915 | bytes 1327293 | solution.py:88
  406.0 7.6 %collective-permute-start.4 = (f32[16,1,128]{2,1,0:T(1,128)S(1)}, f32[16,1,128]{2,1,0:T(1,128)S(1)}, u32[]{:S(2)}, u32[]{:S(2)}) collective-permute-start(f32[16,1,128]{2,1,0:T(1,128)S(1)} %slice.351), channel_id=1, source_target_pairs={{0,1},{1,2},{2,3},{3,4},{4,5},{5,6},{6,7},{7,8},{8,9},{9,10},{10,1... | collective-permute-start | bytes 24584 | tf_op jit(solution)/shard_map/while/body/eval_jaxpr/ppermute | solution.py:20
  419.5 7.3 %collective-permute-start.4 = (f32[16,1,128]{2,1,0:T(1,128)S(1)}, f32[16,1,128]{2,1,0:T(1,128)S(1)}, u32[]{:S(2)}, u32[]{:S(2)}) collective-permute-start(f32[16,1,128]{2,1,0:T(1,128)S(1)} %slice.351), channel_id=1, source_target_pairs={{0,1},{1,2},{2,3},{3,4},{4,5},{5,6},{6,7},{7,8},{8,9},{9,10},{10,1... | collective-permute-start | bytes 24584 | tf_op jit(solution)/shard_map/while/body/eval_jaxpr/ppermute | solution.py:20
  432.7 7.6 %collective-permute-start.4 = (f32[16,1,128]{2,1,0:T(1,128)S(1)}, f32[16,1,128]{2,1,0:T(1,128)S(1)}, u32[]{:S(2)}, u32[]{:S(2)}) collective-permute-start(f32[16,1,128]{2,1,0:T(1,128)S(1)} %slice.351), channel_id=1, source_target_pairs={{0,1},{1,2},{2,3},{3,4},{4,5},{5,6},{6,7},{7,8},{8,9},{9,10},{10,1... | collective-permute-start | bytes 24584 | tf_op jit(solution)/shard_map/while/body/eval_jaxpr/ppermute | solution.py:20
  446.1 7.3 %collective-permute-start.4 = (f32[16,1,128]{2,1,0:T(1,128)S(1)}, f32[16,1,128]{2,1,0:T(1,128)S(1)}, u32[]{:S(2)}, u32[]{:S(2)}) collective-permute-start(f32[16,1,128]{2,1,0:T(1,128)S(1)} %slice.351), channel_id=1, source_target_pairs={{0,1},{1,2},{2,3},{3,4},{4,5},{5,6},{6,7},{7,8},{8,9},{9,10},{10,1... | collective-permute-start | bytes 24584 | tf_op jit(solution)/shard_map/while/body/eval_jaxpr/ppermute | solution.py:20
  455.6 3.6 collective-permute-done.5
  459.3 7.6 %collective-permute-start.4 = (f32[16,1,128]{2,1,0:T(1,128)S(1)}, f32[16,1,128]{2,1,0:T(1,128)S(1)}, u32[]{:S(2)}, u32[]{:S(2)}) collective-permute-start(f32[16,1,128]{2,1,0:T(1,128)S(1)} %slice.351), channel_id=1, source_target_pairs={{0,1},{1,2},{2,3},{3,4},{4,5},{5,6},{6,7},{7,8},{8,9},{9,10},{10,1... | collective-permute-start | bytes 24584 | tf_op jit(solution)/shard_map/while/body/eval_jaxpr/ppermute | solution.py:20
  469.2 3.7 collective-permute-done.5
  473.0 7.2 collective-permute-start.4
  486.2 7.3 %collective-permute-start.4 = (f32[16,1,128]{2,1,0:T(1,128)S(1)}, f32[16,1,128]{2,1,0:T(1,128)S(1)}, u32[]{:S(2)}, u32[]{:S(2)}) collective-permute-start(f32[16,1,128]{2,1,0:T(1,128)S(1)} %slice.351), channel_id=1, source_target_pairs={{0,1},{1,2},{2,3},{3,4},{4,5},{5,6},{6,7},{7,8},{8,9},{9,10},{10,1... | collective-permute-start | bytes 24584 | tf_op jit(solution)/shard_map/while/body/eval_jaxpr/ppermute | solution.py:20
  495.7 4.2 collective-permute-done.5
  500.0 7.0 collective-permute-start.4
  513.7 188.2 %all-gather.4.cloned.1.call-done = f32[16,512,128]{2,1,0:T(8,128)} async-done(((f32[16,8,128]{2,1,0:T(8,128)}), f32[16,512,128]{2,1,0:T(8,128)}) %all-gather.4.cloned.1.call-update) | async-done | bytes 4194320 | tf_op jit(solution)/shard_map/all_gather | solution.py:95
  701.9 4.5 convolution_bitcast_fusion
  707.2 5.3 all_to_all.25
  (367 shorter events, 201.1 us)
Async XLA Ops:
  16.8 16.8 %all-to-all-start = ((f32[2,16,1]{1,2,0:T(1,128)}), f32[2,16,1]{1,2,0:T(1,128)S(1)}, u32[]{:S(2)}, u32[]{:S(2)}) async-start(f32[2,16,1]{1,2,0:T(1,128)} %bitcast.7), calls=%async_computation | async-start | bytes 2048 | tf_op jit(solution)/shard_map/all_to_all | solution.py:130
  38.0 5.5 all-to-all-start.1
  41.5 80.7 %all-gather.6.cloned.1.call-start = ((), (), s32[]{:S(2)}) async-start(), calls=%async_computation.5 | async-start | bytes 4259840 | tf_op jit(solution)/shard_map/all_gather | solution.py:56
  44.9 657.0 %all-gather.4.cloned.1.call-start = ((), (), s32[]{:S(2)}) async-start(), calls=%async_computation.4 | async-start | bytes 4259840 | tf_op jit(solution)/shard_map/all_gather | solution.py:95
  144.6 5.2 collective-permute-start
  154.7 6.3 collective-permute-start
  161.1 4.9 collective-permute-start.1
  166.2 6.3 collective-permute-start
  177.3 6.3 collective-permute-start
  183.7 5.0 collective-permute-start.1
  188.9 5.9 collective-permute-start
  199.7 6.3 collective-permute-start
  211.0 6.3 collective-permute-start.2
  222.2 6.3 collective-permute-start.2
  228.6 4.9 collective-permute-start.3
  233.7 6.3 collective-permute-start.2
  244.8 6.3 collective-permute-start.2
  251.2 5.0 collective-permute-start.3
  256.3 5.9 collective-permute-start.2
  267.2 6.3 collective-permute-start.2
  278.4 6.3 collective-permute-start.2
  289.5 6.3 collective-permute-start.2
  295.9 4.9 collective-permute-start.3
  301.0 6.3 collective-permute-start.6
  307.4 5.2 collective-permute-start.7
  312.8 8.1 %collective-permute-start.6 = (f32[16,1,128]{2,1,0:T(1,128)S(1)}, f32[16,1,128]{2,1,0:T(1,128)S(1)}, u32[]{:S(2)}, u32[]{:S(2)}) collective-permute-start(f32[16,1,128]{2,1,0:T(1,128)S(1)} %slice.355), channel_id=1, source_target_pairs={{0,1},{1,2},{2,3},{3,4},{4,5},{5,6},{6,7},{7,8},{8,9},{9,10},{10,1... | collective-permute-start | bytes 24584 | tf_op jit(solution)/shard_map/while/body/eval_jaxpr/ppermute | solution.py:20
  321.0 5.2 collective-permute-start.7
  326.3 7.8 %collective-permute-start.6 = (f32[16,1,128]{2,1,0:T(1,128)S(1)}, f32[16,1,128]{2,1,0:T(1,128)S(1)}, u32[]{:S(2)}, u32[]{:S(2)}) collective-permute-start(f32[16,1,128]{2,1,0:T(1,128)S(1)} %slice.355), channel_id=1, source_target_pairs={{0,1},{1,2},{2,3},{3,4},{4,5},{5,6},{6,7},{7,8},{8,9},{9,10},{10,1... | collective-permute-start | bytes 24584 | tf_op jit(solution)/shard_map/while/body/eval_jaxpr/ppermute | solution.py:20
  339.0 8.6 %collective-permute-start.6 = (f32[16,1,128]{2,1,0:T(1,128)S(1)}, f32[16,1,128]{2,1,0:T(1,128)S(1)}, u32[]{:S(2)}, u32[]{:S(2)}) collective-permute-start(f32[16,1,128]{2,1,0:T(1,128)S(1)} %slice.355), channel_id=1, source_target_pairs={{0,1},{1,2},{2,3},{3,4},{4,5},{5,6},{6,7},{7,8},{8,9},{9,10},{10,1... | collective-permute-start | bytes 24584 | tf_op jit(solution)/shard_map/while/body/eval_jaxpr/ppermute | solution.py:20
  352.5 8.1 %collective-permute-start.6 = (f32[16,1,128]{2,1,0:T(1,128)S(1)}, f32[16,1,128]{2,1,0:T(1,128)S(1)}, u32[]{:S(2)}, u32[]{:S(2)}) collective-permute-start(f32[16,1,128]{2,1,0:T(1,128)S(1)} %slice.355), channel_id=1, source_target_pairs={{0,1},{1,2},{2,3},{3,4},{4,5},{5,6},{6,7},{7,8},{8,9},{9,10},{10,1... | collective-permute-start | bytes 24584 | tf_op jit(solution)/shard_map/while/body/eval_jaxpr/ppermute | solution.py:20
  365.8 8.4 %collective-permute-start.6 = (f32[16,1,128]{2,1,0:T(1,128)S(1)}, f32[16,1,128]{2,1,0:T(1,128)S(1)}, u32[]{:S(2)}, u32[]{:S(2)}) collective-permute-start(f32[16,1,128]{2,1,0:T(1,128)S(1)} %slice.355), channel_id=1, source_target_pairs={{0,1},{1,2},{2,3},{3,4},{4,5},{5,6},{6,7},{7,8},{8,9},{9,10},{10,1... | collective-permute-start | bytes 24584 | tf_op jit(solution)/shard_map/while/body/eval_jaxpr/ppermute | solution.py:20
  374.3 5.0 collective-permute-start.7
  379.4 8.0 %collective-permute-start.6 = (f32[16,1,128]{2,1,0:T(1,128)S(1)}, f32[16,1,128]{2,1,0:T(1,128)S(1)}, u32[]{:S(2)}, u32[]{:S(2)}) collective-permute-start(f32[16,1,128]{2,1,0:T(1,128)S(1)} %slice.355), channel_id=1, source_target_pairs={{0,1},{1,2},{2,3},{3,4},{4,5},{5,6},{6,7},{7,8},{8,9},{9,10},{10,1... | collective-permute-start | bytes 24584 | tf_op jit(solution)/shard_map/while/body/eval_jaxpr/ppermute | solution.py:20
  387.6 5.0 collective-permute-start.7
  392.6 8.0 %collective-permute-start.6 = (f32[16,1,128]{2,1,0:T(1,128)S(1)}, f32[16,1,128]{2,1,0:T(1,128)S(1)}, u32[]{:S(2)}, u32[]{:S(2)}) collective-permute-start(f32[16,1,128]{2,1,0:T(1,128)S(1)} %slice.355), channel_id=1, source_target_pairs={{0,1},{1,2},{2,3},{3,4},{4,5},{5,6},{6,7},{7,8},{8,9},{9,10},{10,1... | collective-permute-start | bytes 24584 | tf_op jit(solution)/shard_map/while/body/eval_jaxpr/ppermute | solution.py:20
  400.8 4.9 collective-permute-start.7
  406.0 8.4 %collective-permute-start.4 = (f32[16,1,128]{2,1,0:T(1,128)S(1)}, f32[16,1,128]{2,1,0:T(1,128)S(1)}, u32[]{:S(2)}, u32[]{:S(2)}) collective-permute-start(f32[16,1,128]{2,1,0:T(1,128)S(1)} %slice.351), channel_id=1, source_target_pairs={{0,1},{1,2},{2,3},{3,4},{4,5},{5,6},{6,7},{7,8},{8,9},{9,10},{10,1... | collective-permute-start | bytes 24584 | tf_op jit(solution)/shard_map/while/body/eval_jaxpr/ppermute | solution.py:20
  414.5 4.9 collective-permute-start.5
  419.5 8.1 %collective-permute-start.4 = (f32[16,1,128]{2,1,0:T(1,128)S(1)}, f32[16,1,128]{2,1,0:T(1,128)S(1)}, u32[]{:S(2)}, u32[]{:S(2)}) collective-permute-start(f32[16,1,128]{2,1,0:T(1,128)S(1)} %slice.351), channel_id=1, source_target_pairs={{0,1},{1,2},{2,3},{3,4},{4,5},{5,6},{6,7},{7,8},{8,9},{9,10},{10,1... | collective-permute-start | bytes 24584 | tf_op jit(solution)/shard_map/while/body/eval_jaxpr/ppermute | solution.py:20
  432.7 8.4 %collective-permute-start.4 = (f32[16,1,128]{2,1,0:T(1,128)S(1)}, f32[16,1,128]{2,1,0:T(1,128)S(1)}, u32[]{:S(2)}, u32[]{:S(2)}) collective-permute-start(f32[16,1,128]{2,1,0:T(1,128)S(1)} %slice.351), channel_id=1, source_target_pairs={{0,1},{1,2},{2,3},{3,4},{4,5},{5,6},{6,7},{7,8},{8,9},{9,10},{10,1... | collective-permute-start | bytes 24584 | tf_op jit(solution)/shard_map/while/body/eval_jaxpr/ppermute | solution.py:20
  446.1 8.1 %collective-permute-start.4 = (f32[16,1,128]{2,1,0:T(1,128)S(1)}, f32[16,1,128]{2,1,0:T(1,128)S(1)}, u32[]{:S(2)}, u32[]{:S(2)}) collective-permute-start(f32[16,1,128]{2,1,0:T(1,128)S(1)} %slice.351), channel_id=1, source_target_pairs={{0,1},{1,2},{2,3},{3,4},{4,5},{5,6},{6,7},{7,8},{8,9},{9,10},{10,1... | collective-permute-start | bytes 24584 | tf_op jit(solution)/shard_map/while/body/eval_jaxpr/ppermute | solution.py:20
  454.3 4.9 collective-permute-start.5
  459.3 8.4 %collective-permute-start.4 = (f32[16,1,128]{2,1,0:T(1,128)S(1)}, f32[16,1,128]{2,1,0:T(1,128)S(1)}, u32[]{:S(2)}, u32[]{:S(2)}) collective-permute-start(f32[16,1,128]{2,1,0:T(1,128)S(1)} %slice.351), channel_id=1, source_target_pairs={{0,1},{1,2},{2,3},{3,4},{4,5},{5,6},{6,7},{7,8},{8,9},{9,10},{10,1... | collective-permute-start | bytes 24584 | tf_op jit(solution)/shard_map/while/body/eval_jaxpr/ppermute | solution.py:20
  467.8 5.0 collective-permute-start.5
  473.0 8.0 %collective-permute-start.4 = (f32[16,1,128]{2,1,0:T(1,128)S(1)}, f32[16,1,128]{2,1,0:T(1,128)S(1)}, u32[]{:S(2)}, u32[]{:S(2)}) collective-permute-start(f32[16,1,128]{2,1,0:T(1,128)S(1)} %slice.351), channel_id=1, source_target_pairs={{0,1},{1,2},{2,3},{3,4},{4,5},{5,6},{6,7},{7,8},{8,9},{9,10},{10,1... | collective-permute-start | bytes 24584 | tf_op jit(solution)/shard_map/while/body/eval_jaxpr/ppermute | solution.py:20
  486.2 8.1 %collective-permute-start.4 = (f32[16,1,128]{2,1,0:T(1,128)S(1)}, f32[16,1,128]{2,1,0:T(1,128)S(1)}, u32[]{:S(2)}, u32[]{:S(2)}) collective-permute-start(f32[16,1,128]{2,1,0:T(1,128)S(1)} %slice.351), channel_id=1, source_target_pairs={{0,1},{1,2},{2,3},{3,4},{4,5},{5,6},{6,7},{7,8},{8,9},{9,10},{10,1... | collective-permute-start | bytes 24584 | tf_op jit(solution)/shard_map/while/body/eval_jaxpr/ppermute | solution.py:20
  494.4 5.5 collective-permute-start.5
  500.0 7.8 %collective-permute-start.4 = (f32[16,1,128]{2,1,0:T(1,128)S(1)}, f32[16,1,128]{2,1,0:T(1,128)S(1)}, u32[]{:S(2)}, u32[]{:S(2)}) collective-permute-start(f32[16,1,128]{2,1,0:T(1,128)S(1)} %slice.351), channel_id=1, source_target_pairs={{0,1},{1,2},{2,3},{3,4},{4,5},{5,6},{6,7},{7,8},{8,9},{9,10},{10,1... | collective-permute-start | bytes 24584 | tf_op jit(solution)/shard_map/while/body/eval_jaxpr/ppermute | solution.py:20
  (28 other events, 306.0 us)
Sparse Core Ops, SparseCore 0:
  45.7 76.5 all-gather.5
  513.7 188.1 all-gather.3
where the time goes:
time: 724 us; the launch traced here: 721 us
  waiting for transfers between devices  403 us (56%)
  starting transfers between devices  248 us (34%)
  local copies, waits for them, and re-layouts  17.8 us (2%)
  other arithmetic  17.4 us (2%)
  between operations  14.4 us (2%)
  matrix products  8.86 us (1%)
  blocking collectives  8.21 us (1%)
    ppermute x64, starting transfers between devices, passed_along(): return lax.ppermute(block, axis, route)  238 us
    all_gather x1, waiting for transfers between devices, ice_work(): lax.all_gather(adj_z, 'ice', axis=1, tiled=True)  188 us
    ppermute x64, waiting for transfers between devices, passed_along(): return lax.ppermute(block, axis, route)  138 us
    all_gather x1, waiting for transfers between devices, ice_work(): lax.all_gather(source, 'ice', axis=1, tiled=True)  77.3 us
  transfers between devices with their start and end apart: 69, of which 66 were waited for; matrix products, arithmetic and copies ran while one was open for 2% of the time, Pallas kernels for 0%

commit v1 on v0

v1 whole, which is shorter than its diff:
```python
import jax
import jax.numpy as jnp
from jax import lax
from jax.experimental import pallas as pl
from jax.experimental.pallas import tpu as pltpu
from jax.sharding import PartitionSpec as P

PLASTIC = 0.25
VISCOUS = 1.0
GAMMA = 0.6
BETA = 0.9
STEP = 0.04

HALF = 8
BLOCKS = 64
ICE = 64
SLOTS = 16
PARTS = 4
GROUPS = 64
ROWS = 512
F32 = jnp.float32
BF16 = jnp.bfloat16


def vmem():
    return pl.BlockSpec(memory_space=pltpu.VMEM)


def smem():
    return pl.BlockSpec(memory_space=pltpu.SMEM)


def ranked(covered_ref, index_ref):
    def clear(k, carry):
        index_ref[k] = 0
        return carry

    lax.fori_loop(0, BLOCKS, clear, 0)

    def visit(b, count):
        index_ref[count] = b
        return count + covered_ref[b]

    return lax.fori_loop(0, BLOCKS, visit, 0)


def gather_kernel(
    covered_ref, reinit_ref, velo_ref, stress_ref, thick_ref, switch_ref, force_ref, cotu_ref, cots_ref,
    own_ref, send_ref, keep_ref, index_ref,
):
    count = ranked(covered_ref, index_ref)
    heavy = count > 1

    def fields(block):
        coef = jnp.where(switch_ref[block] == 1, PLASTIC, VISCOUS)
        source = thick_ref[block] * coef
        return (velo_ref[block], cotu_ref[block], stress_ref[block], cots_ref[block], force_ref[block], source)

    def keep_row(block):
        return jnp.full((1, 128), 1 - reinit_ref[block], jnp.int32).astype(F32)

    def one_send(k, carry):
        block = index_ref[jnp.where(heavy, SLOTS + k, 0)]
        for f, tile in enumerate(fields(block)):
            send_ref[6 * k + f] = tile
        send_ref[6 * SLOTS + k, 0:1, :] = keep_row(block)
        return carry

    def one_own(k, carry):
        block = index_ref[jnp.where(heavy, k, 0)]
        for f, tile in enumerate(fields(block)):
            own_ref[6 * k + f] = tile
        keep_ref[k, 0:1, :] = keep_row(block)
        return carry

    lax.fori_loop(0, SLOTS - 1, one_send, 0)
    lax.fori_loop(0, SLOTS, one_own, 0)


def pack_kernel(covered_ref, own_ref, got_ref, keep_ref, out_ref, kept_ref):
    def add(b, count):
        return count + covered_ref[b]

    heavy = lax.fori_loop(0, BLOCKS, add, 0) > 1
    lane = lax.broadcasted_iota(jnp.int32, (8, 128), 1)
    low = lane < 64
    spot = lane % 64

    def one(k, carry):
        mine = jnp.logical_or(heavy, k == SLOTS - 1)
        tiles = [jnp.where(mine, own_ref[6 * k + f], got_ref[6 * k + f]) for f in range(6)]
        for q in range(PARTS):
            shift = (16 - 32 * q) % 128
            for t in range(3):
                both = jnp.where(
                    low,
                    pltpu.roll(tiles[2 * t], shift, 1) if shift else tiles[2 * t],
                    pltpu.roll(tiles[2 * t + 1], (shift + 64) % 128, 1),
                )
                if q == 0:
                    both = jnp.where(spot >= 16, both, 0.0)
                if q == PARTS - 1:
                    both = jnp.where(spot < 48, both, 0.0)
                out_ref[PARTS * k + q, pl.ds(8 * t, 8), :] = both
        return carry

    lax.fori_loop(0, SLOTS, one, 0)
    slot = lax.axis_index("ice") // PARTS
    mine = jnp.logical_or(heavy, slot == SLOTS - 1)
    row = jnp.where(mine, keep_ref[slot, 0:1, :], got_ref[6 * SLOTS + slot, 0:1, :])
    kept_ref[...] = jnp.broadcast_to(row, (8, 128))


def product(a, b, dims):
    a_high = a.astype(BF16)
    a_low = (a - a_high.astype(F32)).astype(BF16)
    b_high = b.astype(BF16)
    b_low = (b - b_high.astype(F32)).astype(BF16)

    def dot(x, y):
        return lax.dot_general(x, y, (dims, ((), ())), preferred_element_type=F32)

    return dot(a_low, b_high) + dot(a_high, b_low) + dot(a_high, b_high)


def spread(v):
    return pl.ds(v, 8, stride=GROUPS)


def work_kernel(
    in_ref, kernel_ref, kept_ref, out_ref,
    x_ref, y_ref, zf_ref, zb_ref, f_ref, acc_ref, af_ref, saved_ref, coef_ref, col_ref,
):
    part = lax.axis_index("ice") % PARTS
    lane = lax.broadcasted_iota(jnp.int32, (8, 128), 1)
    sub = lax.broadcasted_iota(jnp.int32, (8, 128), 0)
    low = lane < 64
    edge = jnp.logical_and(lane % 64 == 16, part == 0)

    last = in_ref[:, 16:24, :].reshape(ROWS, 128)
    col_ref[...] = product(kernel_ref[...], last, ((1,), (0,)))

    def load(v, t):
        return in_ref[pl.ds(v // 8, 8, stride=8), 8 * t + v % 8, :]

    for v in range(GROUPS):
        zeta = col_ref[spread(v), :]
        zb_ref[v] = jnp.where(low, -STEP, zeta)
        zf_ref[v] = jnp.where(low, pltpu.roll(zeta, 64, 1), -STEP)
        x_ref[v] = load(v, 0)
        y_ref[v] = load(v, 1)
        f_ref[v] = jnp.where(low, STEP * load(v, 2), 0.0)
        af_ref[v] = jnp.zeros((8, 128), F32)
        acc_ref[v] = jnp.zeros((8, 128), F32)

    gamma = jnp.full((8, 128), GAMMA, F32)
    for j in range(2 * HALF):
        coef_ref[j] = gamma
    coef_ref[0] = jnp.where(low, GAMMA, 1.0)
    coef_ref[HALF] = GAMMA * kept_ref[...]

    def subcycle(j, late):
        coef = coef_ref[j]
        above = jnp.where(sub == 0, 0.0, pltpu.roll(x_ref[GROUPS - 1], 1, 0))
        first_p = None
        held = None
        for v in range(GROUPS + 1):
            if v < GROUPS:
                x = x_ref[v]
                left = jnp.where(edge, 0.0, pltpu.roll(x, 1, 1))
                strain = (x + x) - above - left
                y = coef * y_ref[v] + zf_ref[v] * strain
                p = zb_ref[v] * y
                both = jnp.where(low, strain, y)
                if late:
                    acc_ref[v] += both * saved_ref[2 * HALF - 1 - j, v]
                else:
                    saved_ref[j, v] = pltpu.roll(both, 64, 1)
                y_ref[v] = y
                af_ref[v] += x
                above = x
                if v == 0:
                    first_p = p
                below = p
            else:
                below = jnp.where(sub == 7, 0.0, pltpu.roll(first_p, 7, 0))
            if v > 0:
                old_x, old_p = held
                right = pltpu.roll(old_p, 127, 1)
                x_ref[v - 1] = BETA * old_x + ((old_p + old_p) - below - right) + f_ref[v - 1]
            held = (x, p)

    def early(j, carry):
        subcycle(j, False)
        return carry

    def late(j, carry):
        subcycle(j, True)
        return carry

    lax.fori_loop(0, HALF, early, 0)
    lax.fori_loop(HALF, 2 * HALF, late, 0)

    for v in range(GROUPS):
        total = acc_ref[v]
        col_ref[spread(v), :] = total + pltpu.roll(total, 64, 1)
    adj_q = product(kernel_ref[...], col_ref[...], ((0,), (0,)))
    for v in range(GROUPS):
        tile = jnp.where(
            lane < 32,
            pltpu.roll(x_ref[v], 48, 1),
            jnp.where(lane < 64, GAMMA * pltpu.roll(y_ref[v], 80, 1), STEP * pltpu.roll(af_ref[v], 16, 1)),
        )
        col_ref[spread(v), :] = tile
    here = jnp.logical_and(lane >= 64, lane < 96)[None]
    moved = pltpu.roll(adj_q, 48, 1).reshape(GROUPS, 8, 128)
    result = jnp.where(here, moved, col_ref[...].reshape(GROUPS, 8, 128))
    out_ref[0] = result
    out_ref[1] = result


def unpack_kernel(covered_ref, back_ref, switch_ref, gu_ref, gs_ref, gq_ref, gf_ref, index_ref):
    count = ranked(covered_ref, index_ref)
    heavy = count > 1
    me = lax.axis_index("ocean")
    for ref in (gu_ref, gs_ref, gq_ref, gf_ref):
        ref[...] = jnp.zeros(ref.shape, F32)
    lane = lax.broadcasted_iota(jnp.int32, (8, 128), 1)
    outs = (gu_ref, gs_ref, gq_ref, gf_ref)

    def one(r, carry):
        block = index_ref[r]
        away = r >= SLOTS
        plane = jnp.where(away, 1 - me, me)
        slot = jnp.where(heavy, jnp.where(away, r - SLOTS, r), SLOTS - 1)
        base = plane * ICE + PARTS * slot
        tiles = [back_ref[base + q] for q in range(PARTS)]
        for f in range(4):
            whole = None
            for q in range(PARTS):
                shift = (32 * (q - f)) % 128
                moved = pltpu.roll(tiles[q], shift, 1) if shift else tiles[q]
                whole = moved if q == 0 else jnp.where(lane >= 32 * q, moved, whole)
            if f == 2:
                whole = whole * jnp.where(switch_ref[block] == 1, PLASTIC, VISCOUS)
            outs[f][block] = whole
        return carry

    lax.fori_loop(0, count, one, 0)


def shards(velocity, stress, thickness, forcing, switch, covered, reinit, cot_velocity, cot_stress, kernel):
    tile = (8, 128)

    def sds(*lead):
        return jax.ShapeDtypeStruct(lead + tile, F32)

    params = pltpu.CompilerParams(vmem_limit_bytes=48 * 1024 * 1024)
    own, send, keep = pl.pallas_call(
        gather_kernel,
        name="gather",
        out_shape=(sds(6 * SLOTS), sds(7 * SLOTS), sds(SLOTS)),
        in_specs=[smem(), smem()] + [vmem()] * 7,
        out_specs=(vmem(), vmem(), vmem()),
        scratch_shapes=[pltpu.SMEM((BLOCKS,), jnp.int32)],
        compiler_params=params,
    )(covered, reinit, velocity, stress, thickness, switch, forcing, cot_velocity, cot_stress)
    got = lax.ppermute(send, "ocean", [(0, 1), (1, 0)])
    packed, kept = pl.pallas_call(
        pack_kernel,
        name="pack",
        out_shape=(jax.ShapeDtypeStruct((ICE, 24, 128), F32), sds()),
        in_specs=[smem()] + [vmem()] * 3,
        out_specs=(vmem(), vmem()),
        compiler_params=params,
    )(covered, own, got, keep)
    arrived = lax.all_to_all(packed, "ice", split_axis=0, concat_axis=0, tiled=True)
    col = pltpu.VMEM((GROUPS,) + tile, F32)
    result = pl.pallas_call(
        work_kernel,
        name="work",
        out_shape=sds(2, ICE),
        in_specs=[vmem()] * 3,
        out_specs=vmem(),
        scratch_shapes=[col] * 7
        + [
            pltpu.VMEM((HALF, GROUPS) + tile, F32),
            pltpu.VMEM((2 * HALF,) + tile, F32),
            pltpu.VMEM((ROWS, 128), F32),
        ],
        compiler_params=params,
    )(arrived, kernel, kept)
    back = lax.all_to_all(result.reshape(2 * ICE, 8, 128), ("ocean", "ice"), split_axis=0, concat_axis=0, tiled=True)
    return pl.pallas_call(
        unpack_kernel,
        name="unpack",
        out_shape=(sds(BLOCKS),) * 4,
        in_specs=[smem(), vmem(), vmem()],
        out_specs=(vmem(),) * 4,
        scratch_shapes=[pltpu.SMEM((BLOCKS,), jnp.int32)],
        compiler_params=params,
    )(covered, back, switch)


def solution(mesh):
    cells = P("ocean", "ice", None)
    return jax.shard_map(
        shards,
        mesh=mesh,
        in_specs=(cells, cells, cells, cells, cells, P("ocean"), P("ocean"), cells, cells, P()),
        out_specs=(cells, cells, cells, cells),
        check_vma=False,
    )
```

time: 724 us -> 82.9 us (0.11)
  waiting for transfers between devices: 403 us -> 1.44 us
  starting transfers between devices: 248 us -> 1.5 us
  blocking collectives: 8.21 us -> 44.7 us
  Pallas kernels: 0 us -> 26.2 us
  other arithmetic: 17.4 us -> 0 us
  between operations: 14.4 us -> 0.69 us
  local copies, waits for them, and re-layouts: 17.8 us -> 7.97 us
  matrix products: 8.86 us -> 0 us
    all_gather x2 -> x0, waiting for transfers between devices: 265 us -> none  [the longest x1 188 us: ice_work(): lax.all_gather(adj_z, 'ice', axis=1, tiled=True)]
    ppermute x64 -> x1, starting transfers between devices: 238 us -> 1.5 us  [shards(): got = lax.ppermute(send, 'ocean', [(0, 1), (1, 0)])]
    ppermute x64 -> x1, waiting for transfers between devices: 138 us -> 1.44 us  [shards(): got = lax.ppermute(send, 'ocean', [(0, 1), (1, 0)])]
    all_to_all x1 -> x2, blocking collectives: 5.32 us -> 44.7 us  [the longest x1 26.2 us: shards(): lax.all_to_all(packed, 'ice', split_axis=0, concat_axis=0, tiled=True)]
    pallas_call x0 -> x4, Pallas kernels: none -> 26.2 us  [the longest x1 17.2 us: shards(): pl.pallas_call(work_kernel, name='work', out_shape=sds(2, ICE), in_specs=...]
    all_to_all x3 -> x0, starting transfers between devices: 9.91 us -> none  [the longest x1 3.53 us: shards(): lax.all_to_all(packed, 'ocean', split_axis=0, concat_axis=0, tiled=True)]
    dot_general x2 -> x0, matrix products: 8.86 us -> none  [the longest x1 4.45 us: ice_work(): jnp.einsum('ij,wic->wjc', own_cols, lax.all_gather(adj_z, 'ice', axis=1,...]
  transfers between devices with their start and end apart: 69 -> 1, of which waited for: 66 -> 1; matrix products, arithmetic and copies ran while one was open for 2% -> 0% of each run, Pallas kernels for 0% -> 0%
where the time goes in v1:
time: 82.9 us; the launch traced here: 82.5 us
  blocking collectives  44.7 us (54%)
  Pallas kernels  26.2 us (32%)
  local copies, waits for them, and re-layouts  7.97 us (10%)
  starting transfers between devices  1.5 us (2%)
  waiting for transfers between devices  1.44 us (2%)
    all_to_all x1, blocking collectives, shards(): lax.all_to_all(packed, 'ice', split_axis=0, concat_axis=0, tiled=True)  26.2 us
    all_to_all x1, blocking collectives, shards(): lax.all_to_all(result.reshape(2 * ICE, 8, 128), ('ocean', 'ice'), split_a...  18.5 us
    pallas_call x1, Pallas kernels, shards(): pl.pallas_call(work_kernel, name='work', out_shape=sds(2, ICE), in_specs=...  17.2 us
    unnamed x24, local copies, waits for them, and re-layouts  7.97 us
    pallas_call x1, Pallas kernels, shards(): pl.pallas_call(unpack_kernel, name='unpack', out_shape=(sds(BLOCKS),) * 4...  4.86 us
    pallas_call x1, Pallas kernels, shards(): pl.pallas_call(pack_kernel, name='pack', out_shape=(jax.ShapeDtypeStruct(...  2.44 us
    pallas_call x1, Pallas kernels, shards(): pl.pallas_call(gather_kernel, name='gather', out_shape=(sds(6 * SLOTS), s...  1.71 us
  transfers between devices with their start and end apart: 1, of which 1 were waited for; matrix products, arithmetic and copies ran while one was open for 0% of the time, Pallas kernels for 0%

profile of v1, /device:TPU:1, one launch (start us, length us, event | category | flops | bytes accessed | tf_op | source)
XLA Modules:
  0.0 82.5 jit_solution(13867121630089004801)
XLA Ops:
  0.6 0.0 copy-start.1
  0.6 0.9 %copy-done.1 = s32[64,8,128]{2,1,0:T(8,128)S(1)} copy-done((s32[64,8,128]{2,1,0:T(8,128)S(1)}, s32[64,8,128]{2,1,0:T(8,128)}, u32[]{:S(2)}) %copy-start.1) | copy-done | bytes 262168
  1.6 0.0 copy-start.3
  1.6 0.9 %copy-done.3 = f32[64,8,128]{2,1,0:T(8,128)S(1)} copy-done((f32[64,8,128]{2,1,0:T(8,128)S(1)}, f32[64,8,128]{2,1,0:T(8,128)}, u32[]{:S(2)}) %copy-start.3) | copy-done | bytes 262168
  2.5 0.0 copy-start.4
  2.5 0.9 %copy-done.4 = f32[64,8,128]{2,1,0:T(8,128)S(1)} copy-done((f32[64,8,128]{2,1,0:T(8,128)S(1)}, f32[64,8,128]{2,1,0:T(8,128)}, u32[]{:S(2)}) %copy-start.4) | copy-done | bytes 262168
  3.5 0.0 copy-start.5
  3.5 0.9 %copy-done.5 = f32[64,8,128]{2,1,0:T(8,128)S(1)} copy-done((f32[64,8,128]{2,1,0:T(8,128)S(1)}, f32[64,8,128]{2,1,0:T(8,128)}, u32[]{:S(2)}) %copy-start.5) | copy-done | bytes 262168
  4.4 0.0 copy-start.6
  4.4 0.9 %copy-done.6 = f32[64,8,128]{2,1,0:T(8,128)S(1)} copy-done((f32[64,8,128]{2,1,0:T(8,128)S(1)}, f32[64,8,128]{2,1,0:T(8,128)}, u32[]{:S(2)}) %copy-start.6) | copy-done | bytes 262168
  5.4 0.0 copy-start.7
  5.4 0.9 %copy-done.7 = f32[64,8,128]{2,1,0:T(8,128)S(1)} copy-done((f32[64,8,128]{2,1,0:T(8,128)S(1)}, f32[64,8,128]{2,1,0:T(8,128)}, u32[]{:S(2)}) %copy-start.7) | copy-done | bytes 262168
  6.3 0.0 copy-start.8
  6.3 0.9 %copy-done.8 = f32[64,8,128]{2,1,0:T(8,128)S(1)} copy-done((f32[64,8,128]{2,1,0:T(8,128)S(1)}, f32[64,8,128]{2,1,0:T(8,128)}, u32[]{:S(2)}) %copy-start.8) | copy-done | bytes 262168
  7.3 0.0 copy-start.9
  7.3 0.7 copy-done.9
  7.9 0.0 copy-start.11
  7.9 0.7 copy-done.11
  8.6 1.7 %gather.1 = (f32[96,8,128]{2,1,0:T(8,128)S(1)}, f32[112,8,128]{2,1,0:T(8,128)S(1)}, f32[16,8,128]{2,1,0:T(8,128)S(1)}) custom-call(s32[64]{0:T(128)S(1)} %copy-done.9, s32[64]{0:T(128)S(1)} %copy-done.11, f32[64,8,128]{2,1,0:T(8,128)S(1)} %copy-done.3, f32[64,8,128]{2,1,0:T(8,128)S(1)} %copy-done.4, f32[64,8,128]{2,1,0:T(8,128)S(1)} %copy-done.5, ...), custom_call_target="tpu_custom_call" | custom-call | tf_op jit(solution)/shard_map/gather/pallas_call | solution.py:259
  10.3 1.5 %collective-permute-start = (f32[112,8,128]{2,1,0:T(8,128)S(1)}, f32[112,8,128]{2,1,0:T(8,128)S(1)}, u32[]{:S(2)}, u32[]{:S(2)}) collective-permute-start(f32[112,8,128]{2,1,0:T(8,128)S(1)} %get-tuple-element.10), channel_id=1, source_target_pairs={{0,64},{64,0},{1,65},{65,1},{2,66},{66,2},{3,67},{67,3},{4,68},{68... | collective-permute-start | bytes 1376264 | tf_op jit(solution)/shard_map/ppermute | solution.py:268
  11.8 1.4 %collective-permute-done.got_ref = f32[112,8,128]{2,1,0:T(8,128)S(1)} collective-permute-done((f32[112,8,128]{2,1,0:T(8,128)S(1)}, f32[112,8,128]{2,1,0:T(8,128)S(1)}, u32[]{:S(2)}, u32[]{:S(2)}) %collective-permute-start) | collective-permute-done | bytes 458784 | tf_op jit(solution)/shard_map/ppermute | solution.py:268
  13.3 0.0 copy-start
  13.3 2.4 %pack.1 = (f32[64,24,128]{2,1,0:T(8,128)S(1)}, f32[8,128]{1,0:T(8,128)S(1)}) custom-call(s32[64]{0:T(128)S(1)} %copy-done.9, f32[96,8,128]{2,1,0:T(8,128)S(1)} %get-tuple-element.9.own_ref, f32[112,8,128]{2,1,0:T(8,128)S(1)} %collective-permute-done.got_ref, f32[16,8,128]{2,1,0:T(8,128)S(1)} %get-tuple-element.11.keep_ref), custom_call_target="tpu_custom_call" | custom-call | tf_op jit(solution)/shard_map/pack/pallas_call | solution.py:269
  15.7 26.2 %all_to_all.10.in_ref = f32[64,24,128]{2,1,0:T(8,128)S(1)} all-to-all(f32[64,24,128]{2,1,0:T(8,128)S(1)} %get-tuple-element.12), channel_id=1, replica_groups=mesh['ocean'=2,'ice'=64] {'ice'}, dimensions={0} | all-to-all | bytes 1572864 | tf_op jit(solution)/shard_map/all_to_all | solution.py:277
  41.9 0.0 copy-done
  41.9 17.2 %work.1 = f32[2,64,8,128]{3,2,1,0:T(8,128)S(1)} custom-call(f32[64,24,128]{2,1,0:T(8,128)S(1)} %all_to_all.10.in_ref, f32[512,512]{1,0:T(8,128)S(1)} %copy-done, f32[8,128]{1,0:T(8,128)S(1)} %get-tuple-element.13.kept_ref), custom_call_target="tpu_custom_call" | custom-call | tf_op jit(solution)/shard_map/work/pallas_call | solution.py:279
  59.1 0.0 copy-start.2
  59.1 0.0 copy-start.10
  59.1 18.5 %all_to_all.11.back_ref = f32[128,8,128]{2,1,0:T(8,128)S(1)} all-to-all(f32[128,8,128]{2,1,0:T(8,128)S(1)} %bitcast.1), channel_id=1, replica_groups=mesh['ocean'=2,'ice'=64] {'ocean','ice'}, dimensions={0} | all-to-all | bytes 1048576 | tf_op jit(solution)/shard_map/all_to_all | solution.py:293
  77.6 0.0 copy-done.2
  77.6 0.0 copy-done.10
  77.6 4.9 %unpack.1 = (f32[64,8,128]{2,1,0:T(8,128)}, f32[64,8,128]{2,1,0:T(8,128)}, f32[64,8,128]{2,1,0:T(8,128)}, f32[64,8,128]{2,1,0:T(8,128)}) custom-call(s32[64]{0:T(128)S(1)} %copy-done.10, f32[128,8,128]{2,1,0:T(8,128)S(1)} %all_to_all.11.back_ref, s32[64,8,128]{2,1,0:T(8,128)S(1)} %copy-done.2), custom_call_target="tpu_custom_call" | custom-call | tf_op jit(solution)/shard_map/unpack/pallas_call | solution.py:294
Async XLA Ops:
  0.6 1.0 %copy-start.1 = (s32[64,8,128]{2,1,0:T(8,128)S(1)}, s32[64,8,128]{2,1,0:T(8,128)}, u32[]{:S(2)}) copy-start(s32[64,8,128]{2,1,0:T(8,128)} %switch_ref.3) | copy-start | bytes 786436
  1.6 0.9 %copy-start.3 = (f32[64,8,128]{2,1,0:T(8,128)S(1)}, f32[64,8,128]{2,1,0:T(8,128)}, u32[]{:S(2)}) copy-start(f32[64,8,128]{2,1,0:T(8,128)} %velo_ref.1) | copy-start | bytes 786436
  2.5 0.9 %copy-start.4 = (f32[64,8,128]{2,1,0:T(8,128)S(1)}, f32[64,8,128]{2,1,0:T(8,128)}, u32[]{:S(2)}) copy-start(f32[64,8,128]{2,1,0:T(8,128)} %stress_ref.1) | copy-start | bytes 786436
  3.5 0.9 %copy-start.5 = (f32[64,8,128]{2,1,0:T(8,128)S(1)}, f32[64,8,128]{2,1,0:T(8,128)}, u32[]{:S(2)}) copy-start(f32[64,8,128]{2,1,0:T(8,128)} %thick_ref.1) | copy-start | bytes 786436
  4.4 0.9 %copy-start.6 = (f32[64,8,128]{2,1,0:T(8,128)S(1)}, f32[64,8,128]{2,1,0:T(8,128)}, u32[]{:S(2)}) copy-start(f32[64,8,128]{2,1,0:T(8,128)} %force_ref.1) | copy-start | bytes 786436
  5.4 0.9 %copy-start.7 = (f32[64,8,128]{2,1,0:T(8,128)S(1)}, f32[64,8,128]{2,1,0:T(8,128)}, u32[]{:S(2)}) copy-start(f32[64,8,128]{2,1,0:T(8,128)} %cotu_ref.1) | copy-start | bytes 786436
  6.3 0.9 %copy-start.8 = (f32[64,8,128]{2,1,0:T(8,128)S(1)}, f32[64,8,128]{2,1,0:T(8,128)}, u32[]{:S(2)}) copy-start(f32[64,8,128]{2,1,0:T(8,128)} %cots_ref.1) | copy-start | bytes 786436
  7.3 0.7 copy-start.9
  7.9 0.7 copy-start.11
  10.3 2.9 %collective-permute-start = (f32[112,8,128]{2,1,0:T(8,128)S(1)}, f32[112,8,128]{2,1,0:T(8,128)S(1)}, u32[]{:S(2)}, u32[]{:S(2)}) collective-permute-start(f32[112,8,128]{2,1,0:T(8,128)S(1)} %get-tuple-element.10), channel_id=1, source_target_pairs={{0,64},{64,0},{1,65},{65,1},{2,66},{66,2},{3,67},{67,3},{4,68},{68... | collective-permute-start | bytes 1376264 | tf_op jit(solution)/shard_map/ppermute | solution.py:268
  13.3 28.7 %copy-start = (f32[512,512]{1,0:T(8,128)S(1)}, f32[512,512]{1,0:T(8,128)}, u32[]{:S(2)}) copy-start(f32[512,512]{1,0:T(8,128)} %kernel_ref.1) | copy-start | bytes 3145732
  59.1 18.5 %copy-start.2 = (s32[64,8,128]{2,1,0:T(8,128)S(1)}, s32[64,8,128]{2,1,0:T(8,128)}, u32[]{:S(2)}) copy-start(s32[64,8,128]{2,1,0:T(8,128)} %switch_ref.3) | copy-start | bytes 786436
  59.1 18.5 %copy-start.10 = (s32[64]{0:T(128)S(1)}, s32[64]{0:T(128)}, u32[]{:S(2)}) copy-start(s32[64]{0:T(128)} %covered_ref.5) | copy-start | bytes 772

commit v2 on v1

--- a/solution.py
+++ b/solution.py
@@ -18,6 +18,7 @@
 PARTS = 4
 GROUPS = 64
 ROWS = 512
+MOST = 31
 F32 = jnp.float32
 BF16 = jnp.bfloat16
 
@@ -30,65 +31,68 @@
     return pl.BlockSpec(memory_space=pltpu.SMEM)
 
 
-def ranked(covered_ref, index_ref):
-    def clear(k, carry):
-        index_ref[k] = 0
-        return carry
-
-    lax.fori_loop(0, BLOCKS, clear, 0)
-
-    def visit(b, count):
-        index_ref[count] = b
-        return count + covered_ref[b]
-
-    return lax.fori_loop(0, BLOCKS, visit, 0)
+def ranked(covered_ref, index_ref, empty):
+    for k in range(MOST + 1):
+        index_ref[k] = empty
+    count = jnp.int32(0)
+    for b in range(BLOCKS):
+        flag = covered_ref[b]
+        index_ref[jnp.where(flag == 1, count, MOST)] = b
+        count = count + flag
+    return count
+
+
+def is_heavy(covered_ref):
+    count = covered_ref[0]
+    for b in range(1, BLOCKS):
+        count = count + covered_ref[b]
+    return count > 1
 
 
 def gather_kernel(
-    covered_ref, reinit_ref, velo_ref, stress_ref, thick_ref, switch_ref, force_ref, cotu_ref, cots_ref,
-    own_ref, send_ref, keep_ref, index_ref,
+    covered_hbm, reinit_hbm, velo_hbm, cotu_hbm, stress_hbm, cots_hbm, force_hbm, thick_hbm, switch_hbm,
+    own_ref, send_ref, keep_ref,
+    covered_ref, reinit_ref, velo_ref, cotu_ref, stress_ref, cots_ref, force_ref, thick_ref, switch_ref,
+    index_ref, sems,
 ):
-    count = ranked(covered_ref, index_ref)
-    heavy = count > 1
-
-    def fields(block):
+    sources = (covered_hbm, reinit_hbm, velo_hbm, cotu_hbm, stress_hbm, cots_hbm, force_hbm, thick_hbm, switch_hbm)
+    targets = (covered_ref, reinit_ref, velo_ref, cotu_ref, stress_ref, cots_ref, force_ref, thick_ref, switch_ref)
+    copies = [pltpu.make_async_copy(a, b, sems.at[i]) for i, (a, b) in enumerate(zip(sources, targets))]
+    for copy in copies:
+        copy.start()
+    copies[0].wait()
+    heavy = ranked(covered_ref, index_ref, 0) > 1
+    for copy in copies[1:]:
+        copy.wait()
+
+    def put(block, k, out_ref):
         coef = jnp.where(switch_ref[block] == 1, PLASTIC, VISCOUS)
-        source = thick_ref[block] * coef
-        return (velo_ref[block], cotu_ref[block], stress_ref[block], cots_ref[block], force_ref[block], source)
-
-    def keep_row(block):
+        out_ref[6 * k] = velo_ref[block]
+        out_ref[6 * k + 1] = cotu_ref[block]
+        out_ref[6 * k + 2] = stress_ref[block]
+        out_ref[6 * k + 3] = cots_ref[block]
+        out_ref[6 * k + 4] = force_ref[block]
+        out_ref[6 * k + 5] = thick_ref[block] * coef
         return jnp.full((1, 128), 1 - reinit_ref[block], jnp.int32).astype(F32)
 
-    def one_send(k, carry):
+    for k in range(SLOTS - 1):
         block = index_ref[jnp.where(heavy, SLOTS + k, 0)]
-        for f, tile in enumerate(fields(block)):
-            send_ref[6 * k + f] = tile
-        send_ref[6 * SLOTS + k, 0:1, :] = keep_row(block)
-        return carry
-
-    def one_own(k, carry):
+        send_ref[6 * SLOTS + k // 8, k % 8 : k % 8 + 1, :] = put(block, k, send_ref)
+    for k in range(SLOTS):
         block = index_ref[jnp.where(heavy, k, 0)]
-        for f, tile in enumerate(fields(block)):
-            own_ref[6 * k + f] = tile
-        keep_ref[k, 0:1, :] = keep_row(block)
-        return carry
-
-    lax.fori_loop(0, SLOTS - 1, one_send, 0)
-    lax.fori_loop(0, SLOTS, one_own, 0)
+        keep_ref[k // 8, k % 8 : k % 8 + 1, :] = put(block, k, own_ref)
 
 
 def pack_kernel(covered_ref, own_ref, got_ref, keep_ref, out_ref, kept_ref):
-    def add(b, count):
-        return count + covered_ref[b]
-
-    heavy = lax.fori_loop(0, BLOCKS, add, 0) > 1
+    heavy = is_heavy(covered_ref)
     lane = lax.broadcasted_iota(jnp.int32, (8, 128), 1)
     low = lane < 64
     spot = lane % 64
 
-    def one(k, carry):
-        mine = jnp.logical_or(heavy, k == SLOTS - 1)
-        tiles = [jnp.where(mine, own_ref[6 * k + f], got_ref[6 * k + f]) for f in range(6)]
+    for k in range(SLOTS):
+        tiles = [own_ref[6 * k + f] for f in range(6)]
+        if k < SLOTS - 1:
+            tiles = [jnp.where(heavy, tile, got_ref[6 * k + f]) for f, tile in enumerate(tiles)]
         for q in range(PARTS):
             shift = (16 - 32 * q) % 128
             for t in range(3):
@@ -102,12 +106,12 @@
                 if q == PARTS - 1:
                     both = jnp.where(spot < 48, both, 0.0)
                 out_ref[PARTS * k + q, pl.ds(8 * t, 8), :] = both
-        return carry
-
-    lax.fori_loop(0, SLOTS, one, 0)
     slot = lax.axis_index("ice") // PARTS
     mine = jnp.logical_or(heavy, slot == SLOTS - 1)
-    row = jnp.where(mine, keep_ref[slot, 0:1, :], got_ref[6 * SLOTS + slot, 0:1, :])
+    sub = slot % 8
+    row = jnp.where(
+        mine, keep_ref[slot // 8, pl.ds(sub, 1), :], got_ref[6 * SLOTS + slot // 8, pl.ds(sub, 1), :]
+    )
     kept_ref[...] = jnp.broadcast_to(row, (8, 128))
 
 
@@ -190,16 +194,8 @@
                 x_ref[v - 1] = BETA * old_x + ((old_p + old_p) - below - right) + f_ref[v - 1]
             held = (x, p)
 
-    def early(j, carry):
-        subcycle(j, False)
-        return carry
-
-    def late(j, carry):
-        subcycle(j, True)
-        return carry
-
-    lax.fori_loop(0, HALF, early, 0)
-    lax.fori_loop(HALF, 2 * HALF, late, 0)
+    for j in range(2 * HALF):
+        subcycle(j, j >= HALF)
 
     for v in range(GROUPS):
         total = acc_ref[v]
@@ -219,21 +215,17 @@
     out_ref[1] = result
 
 
-def unpack_kernel(covered_ref, back_ref, switch_ref, gu_ref, gs_ref, gq_ref, gf_ref, index_ref):
-    count = ranked(covered_ref, index_ref)
-    heavy = count > 1
+def unpack_kernel(covered_ref, back_ref, switch_ref, gu_hbm, gs_hbm, gq_hbm, gf_hbm, all_ref, index_ref, sems):
+    heavy = ranked(covered_ref, index_ref, BLOCKS) > 1
     me = lax.axis_index("ocean")
-    for ref in (gu_ref, gs_ref, gq_ref, gf_ref):
-        ref[...] = jnp.zeros(ref.shape, F32)
+    all_ref[...] = jnp.zeros(all_ref.shape, F32)
     lane = lax.broadcasted_iota(jnp.int32, (8, 128), 1)
-    outs = (gu_ref, gs_ref, gq_ref, gf_ref)
-
-    def one(r, carry):
+    for r in range(MOST):
         block = index_ref[r]
-        away = r >= SLOTS
-        plane = jnp.where(away, 1 - me, me)
-        slot = jnp.where(heavy, jnp.where(away, r - SLOTS, r), SLOTS - 1)
-        base = plane * ICE + PARTS * slot
+        if r >= SLOTS:
+            base = (1 - me) * ICE + PARTS * (r - SLOTS)
+        else:
+            base = me * ICE + jnp.where(heavy, PARTS * r, PARTS * (SLOTS - 1))
         tiles = [back_ref[base + q] for q in range(PARTS)]
         for f in range(4):
             whole = None
@@ -242,11 +234,18 @@
                 moved = pltpu.roll(tiles[q], shift, 1) if shift else tiles[q]
                 whole = moved if q == 0 else jnp.where(lane >= 32 * q, moved, whole)
             if f == 2:
-                whole = whole * jnp.where(switch_ref[block] == 1, PLASTIC, VISCOUS)
-            outs[f][block] = whole
-        return carry
-
-    lax.fori_loop(0, count, one, 0)
+                inside = jnp.minimum(block, BLOCKS - 1)
+                whole = whole * jnp.where(switch_ref[inside] == 1, PLASTIC, VISCOUS)
+            all_ref[f, block] = whole
+    copies = []
+    for f, ref in enumerate((gu_hbm, gs_hbm, gq_hbm, gf_hbm)):
+        for part in range(2):
+            rows = pl.ds(part * (BLOCKS // 2), BLOCKS // 2)
+            copies.append(pltpu.make_async_copy(all_ref.at[f, rows], ref.at[rows], sems.at[2 * f + part]))
+    for copy in copies:
+        copy.start()
+    for copy in copies:
+        copy.wait()
 
 
 def shards(velocity, stress, thickness, forcing, switch, covered, reinit, cot_velocity, cot_stress, kernel):
@@ -259,12 +258,14 @@
     own, send, keep = pl.pallas_call(
         gather_kernel,
         name="gather",
-        out_shape=(sds(6 * SLOTS), sds(7 * SLOTS), sds(SLOTS)),
-        in_specs=[smem(), smem()] + [vmem()] * 7,
+        out_shape=(sds(6 * SLOTS), sds(6 * SLOTS + 2), sds(2)),
+        in_specs=[pl.BlockSpec(memory_space=pl.ANY)] * 9,
         out_specs=(vmem(), vmem(), vmem()),
-        scratch_shapes=[pltpu.SMEM((BLOCKS,), jnp.int32)],
+        scratch_shapes=[pltpu.SMEM((BLOCKS,), jnp.int32)] * 2
+        + [pltpu.VMEM((BLOCKS,) + tile, F32)] * 6
+        + [pltpu.VMEM((BLOCKS,) + tile, jnp.int32), pltpu.SMEM((MOST + 1,), jnp.int32), pltpu.SemaphoreType.DMA((9,))],
         compiler_params=params,
-    )(covered, reinit, velocity, stress, thickness, switch, forcing, cot_velocity, cot_stress)
+    )(covered, reinit, velocity, cot_velocity, stress, cot_stress, forcing, thickness, switch)
     got = lax.ppermute(send, "ocean", [(0, 1), (1, 0)])
     packed, kept = pl.pallas_call(
         pack_kernel,
@@ -296,8 +297,12 @@
         name="unpack",
         out_shape=(sds(BLOCKS),) * 4,
         in_specs=[smem(), vmem(), vmem()],
-        out_specs=(vmem(),) * 4,
-        scratch_shapes=[pltpu.SMEM((BLOCKS,), jnp.int32)],
+        out_specs=(pl.BlockSpec(memory_space=pl.ANY),) * 4,
+        scratch_shapes=[
+            pltpu.VMEM((4, BLOCKS + 1) + tile, F32),
+            pltpu.SMEM((MOST + 1,), jnp.int32),
+            pltpu.SemaphoreType.DMA((8,)),
+        ],
         compiler_params=params,
     )(covered, back, switch)
 

time: 82.9 us -> 66.7 us (0.80)
  Pallas kernels: 26.2 us -> 10.1 us
    pallas_call x1, Pallas kernels: 17.2 us -> 5.96 us  [shards(): pl.pallas_call(work_kernel, name='work', out_shape=sds(2, ICE), in_specs=...]
    pallas_call x1, Pallas kernels: 4.86 us -> 2.2 us  [shards(): pl.pallas_call(unpack_kernel, name='unpack', out_shape=(sds(BLOCKS),) * 4...]
    pallas_call x1, Pallas kernels: 2.44 us -> 1.05 us  [shards(): pl.pallas_call(pack_kernel, name='pack', out_shape=(jax.ShapeDtypeStruct(...]
where the time goes in v2:
time: 66.7 us; the launch traced here: 66.3 us
  blocking collectives  44.7 us (67%)
  Pallas kernels  10.1 us (15%)
  local copies, waits for them, and re-layouts  7.97 us (12%)
  starting transfers between devices  1.51 us (2%)
  waiting for transfers between devices  1.36 us (2%)
  between operations  0.69 us (1%)
    all_to_all x1, blocking collectives, shards(): lax.all_to_all(packed, 'ice', split_axis=0, concat_axis=0, tiled=True)  26.2 us
    all_to_all x1, blocking collectives, shards(): lax.all_to_all(result.reshape(2 * ICE, 8, 128), ('ocean', 'ice'), split_a...  18.5 us
    unnamed x24, local copies, waits for them, and re-layouts  7.97 us
    pallas_call x1, Pallas kernels, shards(): pl.pallas_call(work_kernel, name='work', out_shape=sds(2, ICE), in_specs=...  5.96 us
    pallas_call x1, Pallas kernels, shards(): pl.pallas_call(unpack_kernel, name='unpack', out_shape=(sds(BLOCKS),) * 4...  2.2 us
    ppermute x1, starting transfers between devices, shards(): got = lax.ppermute(send, 'ocean', [(0, 1), (1, 0)])  1.51 us
    ppermute x1, waiting for transfers between devices, shards(): got = lax.ppermute(send, 'ocean', [(0, 1), (1, 0)])  1.36 us
  transfers between devices with their start and end apart: 1, of which 1 were waited for; matrix products, arithmetic and copies ran while one was open for 0% of the time, Pallas kernels for 0%

profile of v2, /device:TPU:1, one launch (start us, length us, event | category | flops | bytes accessed | tf_op | source)
XLA Modules:
  0.0 66.3 jit_solution(1788920361104260219)
XLA Ops:
  0.6 0.0 copy-start.1
  0.6 0.9 %copy-done.1 = s32[64,8,128]{2,1,0:T(8,128)S(1)} copy-done((s32[64,8,128]{2,1,0:T(8,128)S(1)}, s32[64,8,128]{2,1,0:T(8,128)}, u32[]{:S(2)}) %copy-start.1) | copy-done | bytes 262168
  1.6 0.0 copy-start.3
  1.6 0.9 %copy-done.3 = f32[64,8,128]{2,1,0:T(8,128)S(1)} copy-done((f32[64,8,128]{2,1,0:T(8,128)S(1)}, f32[64,8,128]{2,1,0:T(8,128)}, u32[]{:S(2)}) %copy-start.3) | copy-done | bytes 262168
  2.5 0.0 copy-start.4
  2.5 0.9 %copy-done.4 = f32[64,8,128]{2,1,0:T(8,128)S(1)} copy-done((f32[64,8,128]{2,1,0:T(8,128)S(1)}, f32[64,8,128]{2,1,0:T(8,128)}, u32[]{:S(2)}) %copy-start.4) | copy-done | bytes 262168
  3.5 0.0 copy-start.5
  3.5 0.9 %copy-done.5 = f32[64,8,128]{2,1,0:T(8,128)S(1)} copy-done((f32[64,8,128]{2,1,0:T(8,128)S(1)}, f32[64,8,128]{2,1,0:T(8,128)}, u32[]{:S(2)}) %copy-start.5) | copy-done | bytes 262168
  4.4 0.0 copy-start.6
  4.4 0.9 %copy-done.6 = f32[64,8,128]{2,1,0:T(8,128)S(1)} copy-done((f32[64,8,128]{2,1,0:T(8,128)S(1)}, f32[64,8,128]{2,1,0:T(8,128)}, u32[]{:S(2)}) %copy-start.6) | copy-done | bytes 262168
  5.4 0.0 copy-start.7
  5.4 0.9 %copy-done.7 = f32[64,8,128]{2,1,0:T(8,128)S(1)} copy-done((f32[64,8,128]{2,1,0:T(8,128)S(1)}, f32[64,8,128]{2,1,0:T(8,128)}, u32[]{:S(2)}) %copy-start.7) | copy-done | bytes 262168
  6.3 0.0 copy-start.8
  6.3 0.9 %copy-done.8 = f32[64,8,128]{2,1,0:T(8,128)S(1)} copy-done((f32[64,8,128]{2,1,0:T(8,128)S(1)}, f32[64,8,128]{2,1,0:T(8,128)}, u32[]{:S(2)}) %copy-start.8) | copy-done | bytes 262168
  7.3 0.0 copy-start.9
  7.3 0.7 copy-done.9
  7.9 0.0 copy-start.11
  7.9 0.7 copy-done.11
  8.6 0.9 %gather.1 = (f32[96,8,128]{2,1,0:T(8,128)S(1)}, f32[98,8,128]{2,1,0:T(8,128)S(1)}, f32[2,8,128]{2,1,0:T(8,128)S(1)}) custom-call(s32[64]{0:T(128)S(1)} %copy-done.9, s32[64]{0:T(128)S(1)} %copy-done.11, f32[64,8,128]{2,1,0:T(8,128)S(1)} %copy-done.3, f32[64,8,128]{2,1,0:T(8,128)S(1)} %copy-done.4, f32[64,8,128]{2,1,0:T(8,128)S(1)} %copy-done.5, ...), custom_call_target="tpu_custom_call" | custom-call | tf_op jit(solution)/shard_map/gather/pallas_call | solution.py:258
  9.5 1.5 %collective-permute-start = (f32[98,8,128]{2,1,0:T(8,128)S(1)}, f32[98,8,128]{2,1,0:T(8,128)S(1)}, u32[]{:S(2)}, u32[]{:S(2)}) collective-permute-start(f32[98,8,128]{2,1,0:T(8,128)S(1)} %get-tuple-element.10), channel_id=1, source_target_pairs={{0,64},{64,0},{1,65},{65,1},{2,66},{66,2},{3,67},{67,3},{4,68},{68... | collective-permute-start | bytes 1204232 | tf_op jit(solution)/shard_map/ppermute | solution.py:269
  11.0 1.4 %collective-permute-done.got_ref = f32[98,8,128]{2,1,0:T(8,128)S(1)} collective-permute-done((f32[98,8,128]{2,1,0:T(8,128)S(1)}, f32[98,8,128]{2,1,0:T(8,128)S(1)}, u32[]{:S(2)}, u32[]{:S(2)}) %collective-permute-start) | collective-permute-done | bytes 401440 | tf_op jit(solution)/shard_map/ppermute | solution.py:269
  12.4 0.0 copy-start
  12.4 1.0 %pack.1 = (f32[64,24,128]{2,1,0:T(8,128)S(1)}, f32[8,128]{1,0:T(8,128)S(1)}) custom-call(s32[64]{0:T(128)S(1)} %copy-done.9, f32[96,8,128]{2,1,0:T(8,128)S(1)} %get-tuple-element.9.own_ref, f32[98,8,128]{2,1,0:T(8,128)S(1)} %collective-permute-done.got_ref, f32[2,8,128]{2,1,0:T(8,128)S(1)} %get-tuple-element.11.keep_ref), custom_call_target="tpu_custom_call" | custom-call | tf_op jit(solution)/shard_map/pack/pallas_call | solution.py:270
  13.4 26.2 %all_to_all.10.in_ref = f32[64,24,128]{2,1,0:T(8,128)S(1)} all-to-all(f32[64,24,128]{2,1,0:T(8,128)S(1)} %get-tuple-element.12), channel_id=1, replica_groups=mesh['ocean'=2,'ice'=64] {'ice'}, dimensions={0} | all-to-all | bytes 1572864 | tf_op jit(solution)/shard_map/all_to_all | solution.py:278
  39.6 0.0 copy-done
  39.6 6.0 %work.1 = f32[2,64,8,128]{3,2,1,0:T(8,128)S(1)} custom-call(f32[64,24,128]{2,1,0:T(8,128)S(1)} %all_to_all.10.in_ref, f32[512,512]{1,0:T(8,128)S(1)} %copy-done, f32[8,128]{1,0:T(8,128)S(1)} %get-tuple-element.13.kept_ref), custom_call_target="tpu_custom_call" | custom-call | tf_op jit(solution)/shard_map/work/pallas_call | solution.py:280
  45.6 0.0 copy-start.2
  45.6 0.0 copy-start.10
  45.6 18.5 %all_to_all.11.back_ref = f32[128,8,128]{2,1,0:T(8,128)S(1)} all-to-all(f32[128,8,128]{2,1,0:T(8,128)S(1)} %bitcast.1), channel_id=1, replica_groups=mesh['ocean'=2,'ice'=64] {'ocean','ice'}, dimensions={0} | all-to-all | bytes 1048576 | tf_op jit(solution)/shard_map/all_to_all | solution.py:294
  64.1 0.0 copy-done.2
  64.1 0.0 copy-done.10
  64.1 2.2 %unpack.1 = (f32[64,8,128]{2,1,0:T(8,128)}, f32[64,8,128]{2,1,0:T(8,128)}, f32[64,8,128]{2,1,0:T(8,128)}, f32[64,8,128]{2,1,0:T(8,128)}) custom-call(s32[64]{0:T(128)S(1)} %copy-done.10, f32[128,8,128]{2,1,0:T(8,128)S(1)} %all_to_all.11.back_ref, s32[64,8,128]{2,1,0:T(8,128)S(1)} %copy-done.2), custom_call_target="tpu_custom_call" | custom-call | tf_op jit(solution)/shard_map/unpack/pallas_call | solution.py:295
Async XLA Ops:
  0.6 1.0 %copy-start.1 = (s32[64,8,128]{2,1,0:T(8,128)S(1)}, s32[64,8,128]{2,1,0:T(8,128)}, u32[]{:S(2)}) copy-start(s32[64,8,128]{2,1,0:T(8,128)} %switch_ref.1) | copy-start | bytes 786436
  1.6 0.9 %copy-start.3 = (f32[64,8,128]{2,1,0:T(8,128)S(1)}, f32[64,8,128]{2,1,0:T(8,128)}, u32[]{:S(2)}) copy-start(f32[64,8,128]{2,1,0:T(8,128)} %velo_hbm.1) | copy-start | bytes 786436
  2.5 0.9 %copy-start.4 = (f32[64,8,128]{2,1,0:T(8,128)S(1)}, f32[64,8,128]{2,1,0:T(8,128)}, u32[]{:S(2)}) copy-start(f32[64,8,128]{2,1,0:T(8,128)} %cotu_hbm.1) | copy-start | bytes 786436
  3.5 0.9 %copy-start.5 = (f32[64,8,128]{2,1,0:T(8,128)S(1)}, f32[64,8,128]{2,1,0:T(8,128)}, u32[]{:S(2)}) copy-start(f32[64,8,128]{2,1,0:T(8,128)} %stress_hbm.1) | copy-start | bytes 786436
  4.4 0.9 %copy-start.6 = (f32[64,8,128]{2,1,0:T(8,128)S(1)}, f32[64,8,128]{2,1,0:T(8,128)}, u32[]{:S(2)}) copy-start(f32[64,8,128]{2,1,0:T(8,128)} %cots_hbm.1) | copy-start | bytes 786436
  5.4 0.9 %copy-start.7 = (f32[64,8,128]{2,1,0:T(8,128)S(1)}, f32[64,8,128]{2,1,0:T(8,128)}, u32[]{:S(2)}) copy-start(f32[64,8,128]{2,1,0:T(8,128)} %force_hbm.1) | copy-start | bytes 786436
  6.3 0.9 %copy-start.8 = (f32[64,8,128]{2,1,0:T(8,128)S(1)}, f32[64,8,128]{2,1,0:T(8,128)}, u32[]{:S(2)}) copy-start(f32[64,8,128]{2,1,0:T(8,128)} %thick_hbm.1) | copy-start | bytes 786436
  7.3 0.7 copy-start.9
  7.9 0.7 copy-start.11
  9.5 2.9 %collective-permute-start = (f32[98,8,128]{2,1,0:T(8,128)S(1)}, f32[98,8,128]{2,1,0:T(8,128)S(1)}, u32[]{:S(2)}, u32[]{:S(2)}) collective-permute-start(f32[98,8,128]{2,1,0:T(8,128)S(1)} %get-tuple-element.10), channel_id=1, source_target_pairs={{0,64},{64,0},{1,65},{65,1},{2,66},{66,2},{3,67},{67,3},{4,68},{68... | collective-permute-start | bytes 1204232 | tf_op jit(solution)/shard_map/ppermute | solution.py:269
  12.4 27.3 %copy-start = (f32[512,512]{1,0:T(8,128)S(1)}, f32[512,512]{1,0:T(8,128)}, u32[]{:S(2)}) copy-start(f32[512,512]{1,0:T(8,128)} %kernel_ref.1) | copy-start | bytes 3145732
  45.6 18.5 %copy-start.2 = (s32[64,8,128]{2,1,0:T(8,128)S(1)}, s32[64,8,128]{2,1,0:T(8,128)}, u32[]{:S(2)}) copy-start(s32[64,8,128]{2,1,0:T(8,128)} %switch_ref.1) | copy-start | bytes 786436
  45.6 18.5 %copy-start.10 = (s32[64]{0:T(128)S(1)}, s32[64]{0:T(128)}, u32[]{:S(2)}) copy-start(s32[64]{0:T(128)} %covered_ref.3) | copy-start | bytes 772

commit v3 on v2

--- a/solution.py
+++ b/solution.py
@@ -259,13 +259,16 @@
         gather_kernel,
         name="gather",
         out_shape=(sds(6 * SLOTS), sds(6 * SLOTS + 2), sds(2)),
-        in_specs=[pl.BlockSpec(memory_space=pl.ANY)] * 9,
+        in_specs=[pl.BlockSpec(memory_space=pltpu.HBM)] * 9,
         out_specs=(vmem(), vmem(), vmem()),
         scratch_shapes=[pltpu.SMEM((BLOCKS,), jnp.int32)] * 2
         + [pltpu.VMEM((BLOCKS,) + tile, F32)] * 6
         + [pltpu.VMEM((BLOCKS,) + tile, jnp.int32), pltpu.SMEM((MOST + 1,), jnp.int32), pltpu.SemaphoreType.DMA((9,))],
         compiler_params=params,
-    )(covered, reinit, velocity, cot_velocity, stress, cot_stress, forcing, thickness, switch)
+    )(*[
+        pltpu.with_memory_space_constraint(x, pltpu.HBM)
+        for x in (covered, reinit, velocity, cot_velocity, stress, cot_stress, forcing, thickness, switch)
+    ])
     got = lax.ppermute(send, "ocean", [(0, 1), (1, 0)])
     packed, kept = pl.pallas_call(
         pack_kernel,
@@ -297,7 +300,7 @@
         name="unpack",
         out_shape=(sds(BLOCKS),) * 4,
         in_specs=[smem(), vmem(), vmem()],
-        out_specs=(pl.BlockSpec(memory_space=pl.ANY),) * 4,
+        out_specs=(pl.BlockSpec(memory_space=pltpu.HBM),) * 4,
         scratch_shapes=[
             pltpu.VMEM((4, BLOCKS + 1) + tile, F32),
             pltpu.SMEM((MOST + 1,), jnp.int32),

time: 66.7 us -> 59.9 us (0.90)
  local copies, waits for them, and re-layouts: 7.97 us -> 0.66 us
  Pallas kernels: 10.1 us -> 10.8 us
    unnamed x24 -> x6, local copies, waits for them, and re-layouts: 7.97 us -> 0.66 us
    pallas_call x1, Pallas kernels: 0.89 us -> 1.63 us  [shards(): pl.pallas_call(gather_kernel, name='gather', out_shape=(sds(6 * SLOTS), s...]
where the time goes in v3:
time: 59.9 us; the launch traced here: 59.7 us
  blocking collectives  44.7 us (75%)
  Pallas kernels  10.8 us (18%)
  starting transfers between devices  1.51 us (3%)
  waiting for transfers between devices  1.36 us (2%)
  local copies, waits for them, and re-layouts  0.66 us (1%)
  between operations  0.66 us (1%)
    all_to_all x1, blocking collectives, shards(): lax.all_to_all(packed, 'ice', split_axis=0, concat_axis=0, tiled=True)  26.2 us
    all_to_all x1, blocking collectives, shards(): lax.all_to_all(result.reshape(2 * ICE, 8, 128), ('ocean', 'ice'), split_a...  18.5 us
    pallas_call x1, Pallas kernels, shards(): pl.pallas_call(work_kernel, name='work', out_shape=sds(2, ICE), in_specs=...  5.96 us
    pallas_call x1, Pallas kernels, shards(): pl.pallas_call(unpack_kernel, name='unpack', out_shape=(sds(BLOCKS),) * 4...  2.19 us
    pallas_call x1, Pallas kernels, shards(): pl.pallas_call(gather_kernel, name='gather', out_shape=(sds(6 * SLOTS), s...  1.63 us
    ppermute x1, starting transfers between devices, shards(): got = lax.ppermute(send, 'ocean', [(0, 1), (1, 0)])  1.51 us
    ppermute x1, waiting for transfers between devices, shards(): got = lax.ppermute(send, 'ocean', [(0, 1), (1, 0)])  1.36 us
  transfers between devices with their start and end apart: 1, of which 1 were waited for; matrix products, arithmetic and copies ran while one was open for 0% of the time, Pallas kernels for 0%

profile of v3, /device:TPU:1, one launch (start us, length us, event | category | flops | bytes accessed | tf_op | source)
XLA Modules:
  0.0 59.7 jit_solution(14020002158083714780)
XLA Ops:
  0.6 1.6 %gather.1 = (f32[96,8,128]{2,1,0:T(8,128)S(1)}, f32[98,8,128]{2,1,0:T(8,128)S(1)}, f32[2,8,128]{2,1,0:T(8,128)S(1)}) custom-call(s32[64]{0:T(128)} %covered_ref.3, s32[64]{0:T(128)} %reinit_hbm.1, f32[64,8,128]{2,1,0:T(8,128)} %velo_hbm.1, f32[64,8,128]{2,1,0:T(8,128)} %cotu_hbm.1, f32[64,8,128]{2,1,0:T(8,128)} %stress_hbm.1, f32[64,8,128]{2,1,0:T(8,128)} %cots_hbm.1, ...), custom_call_target="tpu_custom_call" | custom-call | tf_op jit(solution)/shard_map/gather/pallas_call | solution.py:258
  2.3 1.5 %collective-permute-start = (f32[98,8,128]{2,1,0:T(8,128)S(1)}, f32[98,8,128]{2,1,0:T(8,128)S(1)}, u32[]{:S(2)}, u32[]{:S(2)}) collective-permute-start(f32[98,8,128]{2,1,0:T(8,128)S(1)} %get-tuple-element.10), channel_id=1, source_target_pairs={{0,64},{64,0},{1,65},{65,1},{2,66},{66,2},{3,67},{67,3},{4,68},{68... | collective-permute-start | bytes 1204232 | tf_op jit(solution)/shard_map/ppermute | solution.py:272
  3.8 1.4 %collective-permute-done.got_ref = f32[98,8,128]{2,1,0:T(8,128)S(1)} collective-permute-done((f32[98,8,128]{2,1,0:T(8,128)S(1)}, f32[98,8,128]{2,1,0:T(8,128)S(1)}, u32[]{:S(2)}, u32[]{:S(2)}) %collective-permute-start) | collective-permute-done | bytes 401440 | tf_op jit(solution)/shard_map/ppermute | solution.py:272
  5.1 0.0 copy-start.2
  5.1 0.7 %copy-done.2 = s32[64]{0:T(128)S(1)} copy-done((s32[64]{0:T(128)S(1)}, s32[64]{0:T(128)}, u32[]{:S(2)}) %copy-start.2) | copy-done | bytes 280
  5.8 0.0 copy-start
  5.8 1.0 %pack.1 = (f32[64,24,128]{2,1,0:T(8,128)S(1)}, f32[8,128]{1,0:T(8,128)S(1)}) custom-call(s32[64]{0:T(128)S(1)} %copy-done.2, f32[96,8,128]{2,1,0:T(8,128)S(1)} %get-tuple-element.9.own_ref, f32[98,8,128]{2,1,0:T(8,128)S(1)} %collective-permute-done.got_ref, f32[2,8,128]{2,1,0:T(8,128)S(1)} %get-tuple-element.11.keep_ref), custom_call_target="tpu_custom_call" | custom-call | tf_op jit(solution)/shard_map/pack/pallas_call | solution.py:273
  6.8 26.2 %all_to_all.10.in_ref = f32[64,24,128]{2,1,0:T(8,128)S(1)} all-to-all(f32[64,24,128]{2,1,0:T(8,128)S(1)} %get-tuple-element.12), channel_id=1, replica_groups=mesh['ocean'=2,'ice'=64] {'ice'}, dimensions={0} | all-to-all | bytes 1572864 | tf_op jit(solution)/shard_map/all_to_all | solution.py:281
  33.1 0.0 copy-done
  33.1 6.0 %work.1 = f32[2,64,8,128]{3,2,1,0:T(8,128)S(1)} custom-call(f32[64,24,128]{2,1,0:T(8,128)S(1)} %all_to_all.10.in_ref, f32[512,512]{1,0:T(8,128)S(1)} %copy-done, f32[8,128]{1,0:T(8,128)S(1)} %get-tuple-element.13.kept_ref), custom_call_target="tpu_custom_call" | custom-call | tf_op jit(solution)/shard_map/work/pallas_call | solution.py:283
  39.0 0.0 copy-start.1
  39.0 18.5 %all_to_all.11.back_ref = f32[128,8,128]{2,1,0:T(8,128)S(1)} all-to-all(f32[128,8,128]{2,1,0:T(8,128)S(1)} %bitcast.1), channel_id=1, replica_groups=mesh['ocean'=2,'ice'=64] {'ocean','ice'}, dimensions={0} | all-to-all | bytes 1048576 | tf_op jit(solution)/shard_map/all_to_all | solution.py:297
  57.5 0.0 copy-done.1
  57.5 2.2 %unpack.1 = (f32[64,8,128]{2,1,0:T(8,128)}, f32[64,8,128]{2,1,0:T(8,128)}, f32[64,8,128]{2,1,0:T(8,128)}, f32[64,8,128]{2,1,0:T(8,128)}) custom-call(s32[64]{0:T(128)S(1)} %copy-done.2, f32[128,8,128]{2,1,0:T(8,128)S(1)} %all_to_all.11.back_ref, s32[64,8,128]{2,1,0:T(8,128)S(1)} %copy-done.1), custom_call_target="tpu_custom_call" | custom-call | tf_op jit(solution)/shard_map/unpack/pallas_call | solution.py:298
Async XLA Ops:
  2.3 2.9 %collective-permute-start = (f32[98,8,128]{2,1,0:T(8,128)S(1)}, f32[98,8,128]{2,1,0:T(8,128)S(1)}, u32[]{:S(2)}, u32[]{:S(2)}) collective-permute-start(f32[98,8,128]{2,1,0:T(8,128)S(1)} %get-tuple-element.10), channel_id=1, source_target_pairs={{0,64},{64,0},{1,65},{65,1},{2,66},{66,2},{3,67},{67,3},{4,68},{68... | collective-permute-start | bytes 1204232 | tf_op jit(solution)/shard_map/ppermute | solution.py:272
  5.1 0.7 %copy-start.2 = (s32[64]{0:T(128)S(1)}, s32[64]{0:T(128)}, u32[]{:S(2)}) copy-start(s32[64]{0:T(128)} %covered_ref.3) | copy-start | bytes 772
  5.8 27.3 %copy-start = (f32[512,512]{1,0:T(8,128)S(1)}, f32[512,512]{1,0:T(8,128)}, u32[]{:S(2)}) copy-start(f32[512,512]{1,0:T(8,128)} %kernel_ref.1) | copy-start | bytes 3145732
  39.0 18.5 %copy-start.1 = (s32[64,8,128]{2,1,0:T(8,128)S(1)}, s32[64,8,128]{2,1,0:T(8,128)}, u32[]{:S(2)}) copy-start(s32[64,8,128]{2,1,0:T(8,128)} %switch_ref.1) | copy-start | bytes 786436

commit v4 on v3

--- a/solution.py
+++ b/solution.py
@@ -40,13 +40,6 @@
         index_ref[jnp.where(flag == 1, count, MOST)] = b
         count = count + flag
     return count
-
-
-def is_heavy(covered_ref):
-    count = covered_ref[0]
-    for b in range(1, BLOCKS):
-        count = count + covered_ref[b]
-    return count > 1
 
 
 def gather_kernel(
@@ -62,29 +55,41 @@
         copy.start()
     copies[0].wait()
     heavy = ranked(covered_ref, index_ref, 0) > 1
-    for copy in copies[1:]:
-        copy.wait()
-
-    def put(block, k, out_ref):
+    sent = [index_ref[jnp.where(heavy, SLOTS + k, 0)] for k in range(SLOTS - 1)]
+    owned = [index_ref[jnp.where(heavy, k, 0)] for k in range(SLOTS)]
+    places = [(send_ref, k, block) for k, block in enumerate(sent)] + [(own_ref, k, block) for k, block in enumerate(owned)]
+    keep_ref[2] = jnp.full((8, 128), heavy.astype(jnp.int32), jnp.int32).astype(F32)
+    copies[1].wait()
+    for out_ref, k, block in places:
+        row = jnp.full((1, 128), 1 - reinit_ref[block], jnp.int32).astype(F32)
+        if out_ref is send_ref:
+            send_ref[6 * SLOTS + k // 8, k % 8 : k % 8 + 1, :] = row
+        else:
+            keep_ref[k // 8, k % 8 : k % 8 + 1, :] = row
+    for f in range(5):
+        copies[2 + f].wait()
+        for out_ref, k, block in places:
+            out_ref[6 * k + f] = targets[2 + f][block]
+    copies[7].wait()
+    copies[8].wait()
+    for out_ref, k, block in places:
         coef = jnp.where(switch_ref[block] == 1, PLASTIC, VISCOUS)
-        out_ref[6 * k] = velo_ref[block]
-        out_ref[6 * k + 1] = cotu_ref[block]
-        out_ref[6 * k + 2] = stress_ref[block]
-        out_ref[6 * k + 3] = cots_ref[block]
-        out_ref[6 * k + 4] = force_ref[block]
         out_ref[6 * k + 5] = thick_ref[block] * coef
-        return jnp.full((1, 128), 1 - reinit_ref[block], jnp.int32).astype(F32)
-
-    for k in range(SLOTS - 1):
-        block = index_ref[jnp.where(heavy, SLOTS + k, 0)]
-        send_ref[6 * SLOTS + k // 8, k % 8 : k % 8 + 1, :] = put(block, k, send_ref)
-    for k in range(SLOTS):
-        block = index_ref[jnp.where(heavy, k, 0)]
-        keep_ref[k // 8, k % 8 : k % 8 + 1, :] = put(block, k, own_ref)
-
-
-def pack_kernel(covered_ref, own_ref, got_ref, keep_ref, out_ref, kept_ref):
-    heavy = is_heavy(covered_ref)
+
+
+def split(x):
+    high = x.astype(BF16)
+    return high, (x - high.astype(F32)).astype(BF16)
+
+
+def split_kernel(kernel_ref, halves_ref):
+    whole = kernel_ref[...]
+    halves_ref[0], halves_ref[1] = split(whole)
+    halves_ref[2], halves_ref[3] = split(whole.T)
+
+
+def pack_kernel(own_ref, got_ref, keep_ref, out_ref, kept_ref):
+    heavy = keep_ref[2] > 0.5
     lane = lax.broadcasted_iota(jnp.int32, (8, 128), 1)
     low = lane < 64
     spot = lane % 64
@@ -107,24 +112,21 @@
                     both = jnp.where(spot < 48, both, 0.0)
                 out_ref[PARTS * k + q, pl.ds(8 * t, 8), :] = both
     slot = lax.axis_index("ice") // PARTS
-    mine = jnp.logical_or(heavy, slot == SLOTS - 1)
     sub = slot % 8
-    row = jnp.where(
-        mine, keep_ref[slot // 8, pl.ds(sub, 1), :], got_ref[6 * SLOTS + slot // 8, pl.ds(sub, 1), :]
-    )
-    kept_ref[...] = jnp.broadcast_to(row, (8, 128))
-
-
-def product(a, b, dims):
-    a_high = a.astype(BF16)
-    a_low = (a - a_high.astype(F32)).astype(BF16)
-    b_high = b.astype(BF16)
-    b_low = (b - b_high.astype(F32)).astype(BF16)
+    mine = jnp.broadcast_to(keep_ref[slot // 8, pl.ds(sub, 1), :], (8, 128))
+    other = jnp.broadcast_to(got_ref[6 * SLOTS + slot // 8, pl.ds(sub, 1), :], (8, 128))
+    own_slot = jnp.full((8, 128), slot, jnp.int32) == SLOTS - 1
+    kept_ref[...] = jnp.where(jnp.logical_or(heavy, own_slot), mine, other)
+
+
+def product(a_high, a_low, b):
+    b_high, b_low = split(b)
 
     def dot(x, y):
-        return lax.dot_general(x, y, (dims, ((), ())), preferred_element_type=F32)
-
-    return dot(a_low, b_high) + dot(a_high, b_low) + dot(a_high, b_high)
+        return jnp.dot(x, y, preferred_element_type=F32)
+
+    wide = dot(a_high, jnp.concatenate([b_high, b_low], axis=1))
+    return (dot(a_low, b_high) + wide[:, 128:]) + wide[:, :128]
 
 
 def spread(v):
@@ -132,7 +134,7 @@
 
 
 def work_kernel(
-    in_ref, kernel_ref, kept_ref, out_ref,
+    in_ref, halves_ref, kept_ref, out_ref,
     x_ref, y_ref, zf_ref, zb_ref, f_ref, acc_ref, af_ref, saved_ref, coef_ref, col_ref,
 ):
     part = lax.axis_index("ice") % PARTS
@@ -142,7 +144,7 @@
     edge = jnp.logical_and(lane % 64 == 16, part == 0)
 
     last = in_ref[:, 16:24, :].reshape(ROWS, 128)
-    col_ref[...] = product(kernel_ref[...], last, ((1,), (0,)))
+    col_ref[...] = product(halves_ref[0], halves_ref[1], last)
 
     def load(v, t):
         return in_ref[pl.ds(v // 8, 8, stride=8), 8 * t + v % 8, :]
@@ -200,7 +202,7 @@
     for v in range(GROUPS):
         total = acc_ref[v]
         col_ref[spread(v), :] = total + pltpu.roll(total, 64, 1)
-    adj_q = product(kernel_ref[...], col_ref[...], ((0,), (0,)))
+    adj_q = product(halves_ref[2], halves_ref[3], col_ref[...])
     for v in range(GROUPS):
         tile = jnp.where(
             lane < 32,
@@ -218,32 +220,31 @@
 def unpack_kernel(covered_ref, back_ref, switch_ref, gu_hbm, gs_hbm, gq_hbm, gf_hbm, all_ref, index_ref, sems):
     heavy = ranked(covered_ref, index_ref, BLOCKS) > 1
     me = lax.axis_index("ocean")
-    all_ref[...] = jnp.zeros(all_ref.shape, F32)
     lane = lax.broadcasted_iota(jnp.int32, (8, 128), 1)
-    for r in range(MOST):
-        block = index_ref[r]
-        if r >= SLOTS:
-            base = (1 - me) * ICE + PARTS * (r - SLOTS)
-        else:
-            base = me * ICE + jnp.where(heavy, PARTS * r, PARTS * (SLOTS - 1))
-        tiles = [back_ref[base + q] for q in range(PARTS)]
-        for f in range(4):
+    blocks = [index_ref[r] for r in range(MOST)]
+    copies = []
+    for f, ref in enumerate((gu_hbm, gs_hbm, gf_hbm, gq_hbm)):
+        f = (0, 1, 3, 2)[f]
+        all_ref[f] = jnp.zeros(all_ref.shape[1:], F32)
+        for r, block in enumerate(blocks):
+            if r >= SLOTS:
+                base = (1 - me) * ICE + PARTS * (r - SLOTS)
+            else:
+                base = me * ICE + jnp.where(heavy, PARTS * r, PARTS * (SLOTS - 1))
             whole = None
             for q in range(PARTS):
                 shift = (32 * (q - f)) % 128
-                moved = pltpu.roll(tiles[q], shift, 1) if shift else tiles[q]
+                moved = back_ref[base + q]
+                if shift:
+                    moved = pltpu.roll(moved, shift, 1)
                 whole = moved if q == 0 else jnp.where(lane >= 32 * q, moved, whole)
             if f == 2:
                 inside = jnp.minimum(block, BLOCKS - 1)
                 whole = whole * jnp.where(switch_ref[inside] == 1, PLASTIC, VISCOUS)
             all_ref[f, block] = whole
-    copies = []
-    for f, ref in enumerate((gu_hbm, gs_hbm, gq_hbm, gf_hbm)):
-        for part in range(2):
-            rows = pl.ds(part * (BLOCKS // 2), BLOCKS // 2)
-            copies.append(pltpu.make_async_copy(all_ref.at[f, rows], ref.at[rows], sems.at[2 * f + part]))
-    for copy in copies:
+        copy = pltpu.make_async_copy(all_ref.at[f, pl.ds(0, BLOCKS)], ref, sems.at[f])
         copy.start()
+        copies.append(copy)
     for copy in copies:
         copy.wait()
 
@@ -254,11 +255,11 @@
     def sds(*lead):
         return jax.ShapeDtypeStruct(lead + tile, F32)
 
-    params = pltpu.CompilerParams(vmem_limit_bytes=48 * 1024 * 1024)
+    params = pltpu.CompilerParams(vmem_limit_bytes=12 * 1024 * 1024)
     own, send, keep = pl.pallas_call(
         gather_kernel,
         name="gather",
-        out_shape=(sds(6 * SLOTS), sds(6 * SLOTS + 2), sds(2)),
+        out_shape=(sds(6 * SLOTS), sds(6 * SLOTS + 2), sds(3)),
         in_specs=[pl.BlockSpec(memory_space=pltpu.HBM)] * 9,
         out_specs=(vmem(), vmem(), vmem()),
         scratch_shapes=[pltpu.SMEM((BLOCKS,), jnp.int32)] * 2
@@ -270,14 +271,22 @@
         for x in (covered, reinit, velocity, cot_velocity, stress, cot_stress, forcing, thickness, switch)
     ])
     got = lax.ppermute(send, "ocean", [(0, 1), (1, 0)])
+    halves = pl.pallas_call(
+        split_kernel,
+        name="split",
+        out_shape=jax.ShapeDtypeStruct((4, ROWS, ROWS), BF16),
+        in_specs=[vmem()],
+        out_specs=vmem(),
+        compiler_params=params,
+    )(kernel)
     packed, kept = pl.pallas_call(
         pack_kernel,
         name="pack",
         out_shape=(jax.ShapeDtypeStruct((ICE, 24, 128), F32), sds()),
-        in_specs=[smem()] + [vmem()] * 3,
+        in_specs=[vmem()] * 3,
         out_specs=(vmem(), vmem()),
         compiler_params=params,
-    )(covered, own, got, keep)
+    )(own, got, keep)
     arrived = lax.all_to_all(packed, "ice", split_axis=0, concat_axis=0, tiled=True)
     col = pltpu.VMEM((GROUPS,) + tile, F32)
     result = pl.pallas_call(
@@ -293,7 +302,7 @@
             pltpu.VMEM((ROWS, 128), F32),
         ],
         compiler_params=params,
-    )(arrived, kernel, kept)
+    )(arrived, halves, kept)
     back = lax.all_to_all(result.reshape(2 * ICE, 8, 128), ("ocean", "ice"), split_axis=0, concat_axis=0, tiled=True)
     return pl.pallas_call(
         unpack_kernel,
@@ -304,7 +313,7 @@
         scratch_shapes=[
             pltpu.VMEM((4, BLOCKS + 1) + tile, F32),
             pltpu.SMEM((MOST + 1,), jnp.int32),
-            pltpu.SemaphoreType.DMA((8,)),
+            pltpu.SemaphoreType.DMA((4,)),
         ],
         compiler_params=params,
     )(covered, back, switch)

time: 59.9 us -> 67.9 us (1.13)
  blocking collectives: 44.7 us -> 18.4 us
  waiting for transfers between devices: 1.36 us -> 15 us
  starting transfers between devices: 1.51 us -> 12.7 us
  Pallas kernels: 10.8 us -> 19.6 us
    all_to_all x1 -> x0, blocking collectives: 26.2 us -> none  [shards(): lax.all_to_all(packed, 'ice', split_axis=0, concat_axis=0, tiled=True)]
    all_to_all x0 -> x1, waiting for transfers between devices: none -> 13.6 us  [shards(): lax.all_to_all(packed, 'ice', split_axis=0, concat_axis=0, tiled=True)]
    all_to_all x0 -> x1, starting transfers between devices: none -> 11.2 us  [shards(): lax.all_to_all(packed, 'ice', split_axis=0, concat_axis=0, tiled=True)]
    pallas_call x1, Pallas kernels: 5.96 us -> 14.4 us  [shards(): pl.pallas_call(work_kernel, name='work', out_shape=sds(2, ICE), in_specs=...]
  transfers between devices with their start and end apart: 1 -> 2, of which waited for: 1 -> 2; matrix products, arithmetic and copies ran while one was open for 0% -> 0% of each run, Pallas kernels for 0% -> 1%
where the time goes in v4:
time: 67.9 us; the launch traced here: 67.6 us
  Pallas kernels  19.6 us (29%)
  blocking collectives  18.4 us (27%)
  waiting for transfers between devices  15 us (22%)
  starting transfers between devices  12.7 us (19%)
  local copies, waits for them, and re-layouts  1.23 us (2%)
    all_to_all x1, blocking collectives, shards(): lax.all_to_all(result.reshape(2 * ICE, 8, 128), ('ocean', 'ice'), split_a...  18.4 us
    pallas_call x1, Pallas kernels, shards(): pl.pallas_call(work_kernel, name='work', out_shape=sds(2, ICE), in_specs=...  14.4 us
    all_to_all x1, waiting for transfers between devices, shards(): lax.all_to_all(packed, 'ice', split_axis=0, concat_axis=0, tiled=True)  13.6 us
    all_to_all x1, starting transfers between devices, shards(): lax.all_to_all(packed, 'ice', split_axis=0, concat_axis=0, tiled=True)  11.2 us
    pallas_call x1, Pallas kernels, shards(): pl.pallas_call(unpack_kernel, name='unpack', out_shape=(sds(BLOCKS),) * 4...  1.94 us
    pallas_call x1, Pallas kernels, shards(): pl.pallas_call(gather_kernel, name='gather', out_shape=(sds(6 * SLOTS), s...  1.54 us
    ppermute x1, starting transfers between devices, shards(): got = lax.ppermute(send, 'ocean', [(0, 1), (1, 0)])  1.5 us
    ppermute x1, waiting for transfers between devices, shards(): got = lax.ppermute(send, 'ocean', [(0, 1), (1, 0)])  1.36 us
  transfers between devices with their start and end apart: 2, of which 2 were waited for; matrix products, arithmetic and copies ran while one was open for 0% of the time, Pallas kernels for 1%

profile of v4, /device:TPU:1, one launch (start us, length us, event | category | flops | bytes accessed | tf_op | source)
XLA Modules:
  0.0 67.6 jit_solution(2325698716118902791)
XLA Ops:
  0.6 1.5 %gather.1 = (f32[96,8,128]{2,1,0:T(8,128)S(1)}, f32[98,8,128]{2,1,0:T(8,128)S(1)}, f32[3,8,128]{2,1,0:T(8,128)S(1)}) custom-call(s32[64]{0:T(128)} %covered_ref.1, s32[64]{0:T(128)} %reinit_hbm.1, f32[64,8,128]{2,1,0:T(8,128)} %velo_hbm.1, f32[64,8,128]{2,1,0:T(8,128)} %cotu_hbm.1, f32[64,8,128]{2,1,0:T(8,128)} %stress_hbm.1, f32[64,8,128]{2,1,0:T(8,128)} %cots_hbm.1, ...), custom_call_target="tpu_custom_call" | custom-call | tf_op jit(solution)/shard_map/gather/pallas_call | solution.py:259
  2.2 1.5 %collective-permute-start = (f32[98,8,128]{2,1,0:T(8,128)S(1)}, f32[98,8,128]{2,1,0:T(8,128)S(1)}, u32[]{:S(2)}, u32[]{:S(2)}) collective-permute-start(f32[98,8,128]{2,1,0:T(8,128)S(1)} %get-tuple-element.10), channel_id=1, source_target_pairs={{0,64},{64,0},{1,65},{65,1},{2,66},{66,2},{3,67},{67,3},{4,68},{68... | collective-permute-start | bytes 1204232 | tf_op jit(solution)/shard_map/ppermute | solution.py:273
  3.7 1.4 %collective-permute-done.got_ref = f32[98,8,128]{2,1,0:T(8,128)S(1)} collective-permute-done((f32[98,8,128]{2,1,0:T(8,128)S(1)}, f32[98,8,128]{2,1,0:T(8,128)S(1)}, u32[]{:S(2)}, u32[]{:S(2)}) %collective-permute-start) | collective-permute-done | bytes 401440 | tf_op jit(solution)/shard_map/ppermute | solution.py:273
  5.0 1.4 %pack.1 = (f32[64,24,128]{2,1,0:T(8,128)}, f32[8,128]{1,0:T(8,128)S(1)}) custom-call(f32[96,8,128]{2,1,0:T(8,128)S(1)} %get-tuple-element.9.own_ref, f32[98,8,128]{2,1,0:T(8,128)S(1)} %collective-permute-done.got_ref, f32[3,8,128]{2,1,0:T(8,128)S(1)} %get-tuple-element.11.keep_ref), custom_call_target="tpu_custom_call" | custom-call | tf_op jit(solution)/shard_map/pack/pallas_call | solution.py:282
  6.4 11.2 %all-to-all-start = ((f32[64,24,128]{2,1,0:T(8,128)}), f32[64,24,128]{2,1,0:T(8,128)S(1)}, u32[]{:S(2)}, u32[]{:S(2)}) async-start(f32[64,24,128]{2,1,0:T(8,128)} %get-tuple-element.12), calls=%async_computation | async-start | bytes 1572864 | tf_op jit(solution)/shard_map/all_to_all | solution.py:290
  17.6 0.0 copy-start
  17.6 1.2 %copy-done = f32[512,512]{1,0:T(8,128)S(1)} copy-done((f32[512,512]{1,0:T(8,128)S(1)}, f32[512,512]{1,0:T(8,128)}, u32[]{:S(2)}) %copy-start) | copy-done | bytes 1048600
  18.9 0.3 split.1.halves_ref
  19.2 13.6 %all-to-all-done.in_ref = f32[64,24,128]{2,1,0:T(8,128)S(1)} async-done(((f32[64,24,128]{2,1,0:T(8,128)}), f32[64,24,128]{2,1,0:T(8,128)S(1)}, u32[]{:S(2)}, u32[]{:S(2)}) %all-to-all-start) | async-done | bytes 786464 | tf_op jit(solution)/shard_map/all_to_all | solution.py:290
  32.8 0.0 copy-start.1
  32.8 0.0 copy-start.2
  32.8 14.4 %work.1 = f32[2,64,8,128]{3,2,1,0:T(8,128)S(1)} custom-call(f32[64,24,128]{2,1,0:T(8,128)S(1)} %all-to-all-done.in_ref, bf16[4,512,512]{2,1,0:T(8,128)(2,1)S(1)} %split.1.halves_ref, f32[8,128]{1,0:T(8,128)S(1)} %get-tuple-element.13.kept_ref), custom_call_target="tpu_custom_call" | custom-call | tf_op jit(solution)/shard_map/work/pallas_call | solution.py:292
  47.2 18.4 %all_to_all.10.back_ref = f32[128,8,128]{2,1,0:T(8,128)S(1)} all-to-all(f32[128,8,128]{2,1,0:T(8,128)S(1)} %bitcast.1), channel_id=1, replica_groups=mesh['ocean'=2,'ice'=64] {'ocean','ice'}, dimensions={0} | all-to-all | bytes 1048576 | tf_op jit(solution)/shard_map/all_to_all | solution.py:306
  65.7 0.0 copy-done.1
  65.7 0.0 copy-done.2
  65.7 1.9 %unpack.1 = (f32[64,8,128]{2,1,0:T(8,128)}, f32[64,8,128]{2,1,0:T(8,128)}, f32[64,8,128]{2,1,0:T(8,128)}, f32[64,8,128]{2,1,0:T(8,128)}) custom-call(s32[64]{0:T(128)S(1)} %copy-done.2, f32[128,8,128]{2,1,0:T(8,128)S(1)} %all_to_all.10.back_ref, s32[64,8,128]{2,1,0:T(8,128)S(1)} %copy-done.1), custom_call_target="tpu_custom_call" | custom-call | tf_op jit(solution)/shard_map/unpack/pallas_call | solution.py:307
Async XLA Ops:
  2.2 2.9 %collective-permute-start = (f32[98,8,128]{2,1,0:T(8,128)S(1)}, f32[98,8,128]{2,1,0:T(8,128)S(1)}, u32[]{:S(2)}, u32[]{:S(2)}) collective-permute-start(f32[98,8,128]{2,1,0:T(8,128)S(1)} %get-tuple-element.10), channel_id=1, source_target_pairs={{0,64},{64,0},{1,65},{65,1},{2,66},{66,2},{3,67},{67,3},{4,68},{68... | collective-permute-start | bytes 1204232 | tf_op jit(solution)/shard_map/ppermute | solution.py:273
  6.4 26.4 %all-to-all-start = ((f32[64,24,128]{2,1,0:T(8,128)}), f32[64,24,128]{2,1,0:T(8,128)S(1)}, u32[]{:S(2)}, u32[]{:S(2)}) async-start(f32[64,24,128]{2,1,0:T(8,128)} %get-tuple-element.12), calls=%async_computation | async-start | bytes 1572864 | tf_op jit(solution)/shard_map/all_to_all | solution.py:290
  17.6 1.2 %copy-start = (f32[512,512]{1,0:T(8,128)S(1)}, f32[512,512]{1,0:T(8,128)}, u32[]{:S(2)}) copy-start(f32[512,512]{1,0:T(8,128)} %kernel_ref.1) | copy-start | bytes 3145732
  32.8 32.8 %copy-start.1 = (s32[64,8,128]{2,1,0:T(8,128)S(1)}, s32[64,8,128]{2,1,0:T(8,128)}, u32[]{:S(2)}) copy-start(s32[64,8,128]{2,1,0:T(8,128)} %switch_ref.1) | copy-start | bytes 786436
  32.8 32.8 %copy-start.2 = (s32[64]{0:T(128)S(1)}, s32[64]{0:T(128)}, u32[]{:S(2)}) copy-start(s32[64]{0:T(128)} %covered_ref.1) | copy-start | bytes 772

commit v5 on v4

--- a/solution.py
+++ b/solution.py
@@ -174,14 +174,14 @@
             if v < GROUPS:
                 x = x_ref[v]
                 left = jnp.where(edge, 0.0, pltpu.roll(x, 1, 1))
-                strain = (x + x) - above - left
+                strain = 2.0 * x - (above + left)
                 y = coef * y_ref[v] + zf_ref[v] * strain
                 p = zb_ref[v] * y
                 both = jnp.where(low, strain, y)
                 if late:
-                    acc_ref[v] += both * saved_ref[2 * HALF - 1 - j, v]
+                    acc_ref[v] += both * pltpu.roll(saved_ref[2 * HALF - 1 - j, v], 64, 1)
                 else:
-                    saved_ref[j, v] = pltpu.roll(both, 64, 1)
+                    saved_ref[j, v] = both
                 y_ref[v] = y
                 af_ref[v] += x
                 above = x
@@ -193,7 +193,7 @@
             if v > 0:
                 old_x, old_p = held
                 right = pltpu.roll(old_p, 127, 1)
-                x_ref[v - 1] = BETA * old_x + ((old_p + old_p) - below - right) + f_ref[v - 1]
+                x_ref[v - 1] = BETA * old_x + (2.0 * old_p - (below + right)) + f_ref[v - 1]
             held = (x, p)
 
     for j in range(2 * HALF):

time: 67.9 us -> 58.6 us (0.86)
  Pallas kernels: 19.6 us -> 10.3 us
    pallas_call x1, Pallas kernels: 14.4 us -> 5.07 us  [shards(): pl.pallas_call(work_kernel, name='work', out_shape=sds(2, ICE), in_specs=...]
where the time goes in v5:
time: 58.6 us; the launch traced here: 58.3 us
  blocking collectives  18.4 us (31%)
  waiting for transfers between devices  15 us (26%)
  starting transfers between devices  12.7 us (22%)
  Pallas kernels  10.3 us (18%)
  local copies, waits for them, and re-layouts  1.23 us (2%)
  between operations  0.67 us (1%)
    all_to_all x1, blocking collectives, shards(): lax.all_to_all(result.reshape(2 * ICE, 8, 128), ('ocean', 'ice'), split_a...  18.4 us
    all_to_all x1, waiting for transfers between devices, shards(): lax.all_to_all(packed, 'ice', split_axis=0, concat_axis=0, tiled=True)  13.6 us
    all_to_all x1, starting transfers between devices, shards(): lax.all_to_all(packed, 'ice', split_axis=0, concat_axis=0, tiled=True)  11.2 us
    pallas_call x1, Pallas kernels, shards(): pl.pallas_call(work_kernel, name='work', out_shape=sds(2, ICE), in_specs=...  5.07 us
    pallas_call x1, Pallas kernels, shards(): pl.pallas_call(unpack_kernel, name='unpack', out_shape=(sds(BLOCKS),) * 4...  1.94 us
    pallas_call x1, Pallas kernels, shards(): pl.pallas_call(gather_kernel, name='gather', out_shape=(sds(6 * SLOTS), s...  1.54 us
    ppermute x1, starting transfers between devices, shards(): got = lax.ppermute(send, 'ocean', [(0, 1), (1, 0)])  1.5 us
    ppermute x1, waiting for transfers between devices, shards(): got = lax.ppermute(send, 'ocean', [(0, 1), (1, 0)])  1.36 us
  transfers between devices with their start and end apart: 2, of which 2 were waited for; matrix products, arithmetic and copies ran while one was open for 0% of the time, Pallas kernels for 1%

profile of v5, /device:TPU:1, one launch (start us, length us, event | category | flops | bytes accessed | tf_op | source)
XLA Modules:
  0.0 58.3 jit_solution(11124989734276824548)
XLA Ops:
  0.6 1.5 %gather.1 = (f32[96,8,128]{2,1,0:T(8,128)S(1)}, f32[98,8,128]{2,1,0:T(8,128)S(1)}, f32[3,8,128]{2,1,0:T(8,128)S(1)}) custom-call(s32[64]{0:T(128)} %covered_ref.1, s32[64]{0:T(128)} %reinit_hbm.1, f32[64,8,128]{2,1,0:T(8,128)} %velo_hbm.1, f32[64,8,128]{2,1,0:T(8,128)} %cotu_hbm.1, f32[64,8,128]{2,1,0:T(8,128)} %stress_hbm.1, f32[64,8,128]{2,1,0:T(8,128)} %cots_hbm.1, ...), custom_call_target="tpu_custom_call" | custom-call | tf_op jit(solution)/shard_map/gather/pallas_call | solution.py:259
  2.2 1.5 %collective-permute-start = (f32[98,8,128]{2,1,0:T(8,128)S(1)}, f32[98,8,128]{2,1,0:T(8,128)S(1)}, u32[]{:S(2)}, u32[]{:S(2)}) collective-permute-start(f32[98,8,128]{2,1,0:T(8,128)S(1)} %get-tuple-element.10), channel_id=1, source_target_pairs={{0,64},{64,0},{1,65},{65,1},{2,66},{66,2},{3,67},{67,3},{4,68},{68... | collective-permute-start | bytes 1204232 | tf_op jit(solution)/shard_map/ppermute | solution.py:273
  3.7 1.4 %collective-permute-done.got_ref = f32[98,8,128]{2,1,0:T(8,128)S(1)} collective-permute-done((f32[98,8,128]{2,1,0:T(8,128)S(1)}, f32[98,8,128]{2,1,0:T(8,128)S(1)}, u32[]{:S(2)}, u32[]{:S(2)}) %collective-permute-start) | collective-permute-done | bytes 401440 | tf_op jit(solution)/shard_map/ppermute | solution.py:273
  5.0 1.4 %pack.1 = (f32[64,24,128]{2,1,0:T(8,128)}, f32[8,128]{1,0:T(8,128)S(1)}) custom-call(f32[96,8,128]{2,1,0:T(8,128)S(1)} %get-tuple-element.9.own_ref, f32[98,8,128]{2,1,0:T(8,128)S(1)} %collective-permute-done.got_ref, f32[3,8,128]{2,1,0:T(8,128)S(1)} %get-tuple-element.11.keep_ref), custom_call_target="tpu_custom_call" | custom-call | tf_op jit(solution)/shard_map/pack/pallas_call | solution.py:282
  6.4 11.2 %all-to-all-start = ((f32[64,24,128]{2,1,0:T(8,128)}), f32[64,24,128]{2,1,0:T(8,128)S(1)}, u32[]{:S(2)}, u32[]{:S(2)}) async-start(f32[64,24,128]{2,1,0:T(8,128)} %get-tuple-element.12), calls=%async_computation | async-start | bytes 1572864 | tf_op jit(solution)/shard_map/all_to_all | solution.py:290
  17.6 0.0 copy-start
  17.6 1.2 %copy-done = f32[512,512]{1,0:T(8,128)S(1)} copy-done((f32[512,512]{1,0:T(8,128)S(1)}, f32[512,512]{1,0:T(8,128)}, u32[]{:S(2)}) %copy-start) | copy-done | bytes 1048600
  18.9 0.3 split.1.halves_ref
  19.2 13.6 %all-to-all-done.in_ref = f32[64,24,128]{2,1,0:T(8,128)S(1)} async-done(((f32[64,24,128]{2,1,0:T(8,128)}), f32[64,24,128]{2,1,0:T(8,128)S(1)}, u32[]{:S(2)}, u32[]{:S(2)}) %all-to-all-start) | async-done | bytes 786464 | tf_op jit(solution)/shard_map/all_to_all | solution.py:290
  32.8 0.0 copy-start.1
  32.8 0.0 copy-start.2
  32.8 5.1 %work.1 = f32[2,64,8,128]{3,2,1,0:T(8,128)S(1)} custom-call(f32[64,24,128]{2,1,0:T(8,128)S(1)} %all-to-all-done.in_ref, bf16[4,512,512]{2,1,0:T(8,128)(2,1)S(1)} %split.1.halves_ref, f32[8,128]{1,0:T(8,128)S(1)} %get-tuple-element.13.kept_ref), custom_call_target="tpu_custom_call" | custom-call | tf_op jit(solution)/shard_map/work/pallas_call | solution.py:292
  37.9 18.4 %all_to_all.10.back_ref = f32[128,8,128]{2,1,0:T(8,128)S(1)} all-to-all(f32[128,8,128]{2,1,0:T(8,128)S(1)} %bitcast.1), channel_id=1, replica_groups=mesh['ocean'=2,'ice'=64] {'ocean','ice'}, dimensions={0} | all-to-all | bytes 1048576 | tf_op jit(solution)/shard_map/all_to_all | solution.py:306
  56.3 0.0 copy-done.1
  56.3 0.0 copy-done.2
  56.3 1.9 %unpack.1 = (f32[64,8,128]{2,1,0:T(8,128)}, f32[64,8,128]{2,1,0:T(8,128)}, f32[64,8,128]{2,1,0:T(8,128)}, f32[64,8,128]{2,1,0:T(8,128)}) custom-call(s32[64]{0:T(128)S(1)} %copy-done.2, f32[128,8,128]{2,1,0:T(8,128)S(1)} %all_to_all.10.back_ref, s32[64,8,128]{2,1,0:T(8,128)S(1)} %copy-done.1), custom_call_target="tpu_custom_call" | custom-call | tf_op jit(solution)/shard_map/unpack/pallas_call | solution.py:307
Async XLA Ops:
  2.2 2.9 %collective-permute-start = (f32[98,8,128]{2,1,0:T(8,128)S(1)}, f32[98,8,128]{2,1,0:T(8,128)S(1)}, u32[]{:S(2)}, u32[]{:S(2)}) collective-permute-start(f32[98,8,128]{2,1,0:T(8,128)S(1)} %get-tuple-element.10), channel_id=1, source_target_pairs={{0,64},{64,0},{1,65},{65,1},{2,66},{66,2},{3,67},{67,3},{4,68},{68... | collective-permute-start | bytes 1204232 | tf_op jit(solution)/shard_map/ppermute | solution.py:273
  6.4 26.4 %all-to-all-start = ((f32[64,24,128]{2,1,0:T(8,128)}), f32[64,24,128]{2,1,0:T(8,128)S(1)}, u32[]{:S(2)}, u32[]{:S(2)}) async-start(f32[64,24,128]{2,1,0:T(8,128)} %get-tuple-element.12), calls=%async_computation | async-start | bytes 1572864 | tf_op jit(solution)/shard_map/all_to_all | solution.py:290
  17.6 1.2 %copy-start = (f32[512,512]{1,0:T(8,128)S(1)}, f32[512,512]{1,0:T(8,128)}, u32[]{:S(2)}) copy-start(f32[512,512]{1,0:T(8,128)} %kernel_ref.1) | copy-start | bytes 3145732
  32.8 23.5 %copy-start.1 = (s32[64,8,128]{2,1,0:T(8,128)S(1)}, s32[64,8,128]{2,1,0:T(8,128)}, u32[]{:S(2)}) copy-start(s32[64,8,128]{2,1,0:T(8,128)} %switch_ref.1) | copy-start | bytes 786436
  32.8 23.5 %copy-start.2 = (s32[64]{0:T(128)S(1)}, s32[64]{0:T(128)}, u32[]{:S(2)}) copy-start(s32[64]{0:T(128)} %covered_ref.1) | copy-start | bytes 772

commit v6 on v5

--- a/solution.py
+++ b/solution.py
@@ -213,35 +213,39 @@
     here = jnp.logical_and(lane >= 64, lane < 96)[None]
     moved = pltpu.roll(adj_q, 48, 1).reshape(GROUPS, 8, 128)
     result = jnp.where(here, moved, col_ref[...].reshape(GROUPS, 8, 128))
-    out_ref[0] = result
-    out_ref[1] = result
-
-
-def unpack_kernel(covered_ref, back_ref, switch_ref, gu_hbm, gs_hbm, gq_hbm, gf_hbm, all_ref, index_ref, sems):
+    out_ref[...] = result
+
+
+def unpack(back_ref, switch_ref, all_ref, f, base, block):
+    lane = lax.broadcasted_iota(jnp.int32, (8, 128), 1)
+    whole = None
+    for q in range(PARTS):
+        shift = (32 * (q - f)) % 128
+        moved = back_ref[base + q]
+        if shift:
+            moved = pltpu.roll(moved, shift, 1)
+        whole = moved if q == 0 else jnp.where(lane >= 32 * q, moved, whole)
+    if f == 2:
+        inside = jnp.minimum(block, BLOCKS - 1)
+        whole = whole * jnp.where(switch_ref[inside] == 1, PLASTIC, VISCOUS)
+    all_ref[f, block] = whole
+
+
+def near_kernel(covered_ref, back_ref, switch_ref, all_ref, index_ref):
     heavy = ranked(covered_ref, index_ref, BLOCKS) > 1
-    me = lax.axis_index("ocean")
-    lane = lax.broadcasted_iota(jnp.int32, (8, 128), 1)
-    blocks = [index_ref[r] for r in range(MOST)]
-    copies = []
-    for f, ref in enumerate((gu_hbm, gs_hbm, gf_hbm, gq_hbm)):
-        f = (0, 1, 3, 2)[f]
+    blocks = [index_ref[r] for r in range(SLOTS)]
+    for f in range(4):
         all_ref[f] = jnp.zeros(all_ref.shape[1:], F32)
         for r, block in enumerate(blocks):
-            if r >= SLOTS:
-                base = (1 - me) * ICE + PARTS * (r - SLOTS)
-            else:
-                base = me * ICE + jnp.where(heavy, PARTS * r, PARTS * (SLOTS - 1))
-            whole = None
-            for q in range(PARTS):
-                shift = (32 * (q - f)) % 128
-                moved = back_ref[base + q]
-                if shift:
-                    moved = pltpu.roll(moved, shift, 1)
-                whole = moved if q == 0 else jnp.where(lane >= 32 * q, moved, whole)
-            if f == 2:
-                inside = jnp.minimum(block, BLOCKS - 1)
-                whole = whole * jnp.where(switch_ref[inside] == 1, PLASTIC, VISCOUS)
-            all_ref[f, block] = whole
+            base = jnp.where(heavy, PARTS * r, PARTS * (SLOTS - 1))
+            unpack(back_ref, switch_ref, all_ref, f, base, block)
+
+
+def far_kernel(index_ref, far_ref, switch_ref, near_ref, gu_hbm, gs_hbm, gq_hbm, gf_hbm, all_ref, sems):
+    copies = []
+    for f, ref in ((0, gu_hbm), (1, gs_hbm), (3, gf_hbm), (2, gq_hbm)):
+        for r in range(SLOTS, MOST):
+            unpack(far_ref, switch_ref, all_ref, f, PARTS * (r - SLOTS), index_ref[r])
         copy = pltpu.make_async_copy(all_ref.at[f, pl.ds(0, BLOCKS)], ref, sems.at[f])
         copy.start()
         copies.append(copy)
@@ -292,7 +296,7 @@
     result = pl.pallas_call(
         work_kernel,
         name="work",
-        out_shape=sds(2, ICE),
+        out_shape=sds(ICE),
         in_specs=[vmem()] * 3,
         out_specs=vmem(),
         scratch_shapes=[col] * 7
@@ -303,20 +307,27 @@
         ],
         compiler_params=params,
     )(arrived, halves, kept)
-    back = lax.all_to_all(result.reshape(2 * ICE, 8, 128), ("ocean", "ice"), split_axis=0, concat_axis=0, tiled=True)
-    return pl.pallas_call(
-        unpack_kernel,
-        name="unpack",
-        out_shape=(sds(BLOCKS),) * 4,
+    back = lax.all_to_all(result, "ice", split_axis=0, concat_axis=0, tiled=True)
+    far = lax.ppermute(back, "ocean", [(0, 1), (1, 0)])
+    near, index = pl.pallas_call(
+        near_kernel,
+        name="near",
+        out_shape=(sds(4, BLOCKS + 1), jax.ShapeDtypeStruct((MOST + 1,), jnp.int32)),
         in_specs=[smem(), vmem(), vmem()],
-        out_specs=(pl.BlockSpec(memory_space=pltpu.HBM),) * 4,
-        scratch_shapes=[
-            pltpu.VMEM((4, BLOCKS + 1) + tile, F32),
-            pltpu.SMEM((MOST + 1,), jnp.int32),
-            pltpu.SemaphoreType.DMA((4,)),
-        ],
+        out_specs=(vmem(), smem()),
         compiler_params=params,
     )(covered, back, switch)
+    outs = pl.pallas_call(
+        far_kernel,
+        name="far",
+        out_shape=(sds(BLOCKS),) * 4 + (sds(4, BLOCKS + 1),),
+        in_specs=[smem()] + [vmem()] * 3,
+        out_specs=(pl.BlockSpec(memory_space=pltpu.HBM),) * 4 + (vmem(),),
+        scratch_shapes=[pltpu.SemaphoreType.DMA((4,))],
+        input_output_aliases={3: 4},
+        compiler_params=params,
+    )(index, far, switch, near)
+    return outs[:4]
 
 
 def solution(mesh):

time: 58.6 us -> 58.3 us (level)
  blocking collectives: 18.4 us -> 13.9 us
  starting transfers between devices: 12.7 us -> 15.8 us
  Pallas kernels: 10.3 us -> 11.5 us
    all_to_all x1, blocking collectives: 18.4 us -> 13.9 us  [shards(): lax.all_to_all(result, 'ice', split_axis=0, concat_axis=0, tiled=True)]
    ppermute x0 -> x1, starting transfers between devices: none -> 3.05 us  [shards(): far = lax.ppermute(back, 'ocean', [(0, 1), (1, 0)])]
    pallas_call x2 -> x3, Pallas kernels: 7.01 us -> 8.24 us  [the longest x1 5.07 us: shards(): pl.pallas_call(work_kernel, name='work', out_shape=sds(ICE), in_specs=[vm...]
  transfers between devices with their start and end apart: 2 -> 3, of which waited for: 2 -> 2; matrix products, arithmetic and copies ran while one was open for 0% -> 0% of each run, Pallas kernels for 1% -> 3%
where the time goes in v6:
time: 58.3 us; the launch traced here: 58 us
  starting transfers between devices  15.8 us (27%)
  waiting for transfers between devices  15 us (26%)
  blocking collectives  13.9 us (24%)
  Pallas kernels  11.5 us (20%)
  local copies, waits for them, and re-layouts  1.23 us (2%)
  between operations  0.69 us (1%)
    all_to_all x1, blocking collectives, shards(): lax.all_to_all(result, 'ice', split_axis=0, concat_axis=0, tiled=True)  13.9 us
    all_to_all x1, waiting for transfers between devices, shards(): lax.all_to_all(packed, 'ice', split_axis=0, concat_axis=0, tiled=True)  13.6 us
    all_to_all x1, starting transfers between devices, shards(): lax.all_to_all(packed, 'ice', split_axis=0, concat_axis=0, tiled=True)  11.2 us
    pallas_call x1, Pallas kernels, shards(): pl.pallas_call(work_kernel, name='work', out_shape=sds(ICE), in_specs=[vm...  5.07 us
    ppermute x1, starting transfers between devices, shards(): far = lax.ppermute(back, 'ocean', [(0, 1), (1, 0)])  3.05 us
    pallas_call x1, Pallas kernels, shards(): pl.pallas_call(far_kernel, name='far', out_shape=(sds(BLOCKS),) * 4 + (sd...  1.65 us
    pallas_call x1, Pallas kernels, shards(): pl.pallas_call(gather_kernel, name='gather', out_shape=(sds(6 * SLOTS), s...  1.54 us
    pallas_call x1, Pallas kernels, shards(): pl.pallas_call(near_kernel, name='near', out_shape=(sds(4, BLOCKS + 1), j...  1.52 us
  transfers between devices with their start and end apart: 3, of which 2 were waited for; matrix products, arithmetic and copies ran while one was open for 0% of the time, Pallas kernels for 3%

profile of v6, /device:TPU:1, one launch (start us, length us, event | category | flops | bytes accessed | tf_op | source)
XLA Modules:
  0.0 58.0 jit_solution(5260570849383535838)
XLA Ops:
  0.6 1.5 %gather.1 = (f32[96,8,128]{2,1,0:T(8,128)S(1)}, f32[98,8,128]{2,1,0:T(8,128)S(1)}, f32[3,8,128]{2,1,0:T(8,128)S(1)}) custom-call(s32[64]{0:T(128)} %covered_ref.1, s32[64]{0:T(128)} %reinit_hbm.1, f32[64,8,128]{2,1,0:T(8,128)} %velo_hbm.1, f32[64,8,128]{2,1,0:T(8,128)} %cotu_hbm.1, f32[64,8,128]{2,1,0:T(8,128)} %stress_hbm.1, f32[64,8,128]{2,1,0:T(8,128)} %cots_hbm.1, ...), custom_call_target="tpu_custom_call" | custom-call | tf_op jit(solution)/shard_map/gather/pallas_call | solution.py:263
  2.2 1.5 %collective-permute-start = (f32[98,8,128]{2,1,0:T(8,128)S(1)}, f32[98,8,128]{2,1,0:T(8,128)S(1)}, u32[]{:S(2)}, u32[]{:S(2)}) collective-permute-start(f32[98,8,128]{2,1,0:T(8,128)S(1)} %get-tuple-element.16), channel_id=1, source_target_pairs={{0,64},{64,0},{1,65},{65,1},{2,66},{66,2},{3,67},{67,3},{4,68},{68... | collective-permute-start | bytes 1204232 | tf_op jit(solution)/shard_map/ppermute | solution.py:277
  3.7 1.4 %collective-permute-done.got_ref = f32[98,8,128]{2,1,0:T(8,128)S(1)} collective-permute-done((f32[98,8,128]{2,1,0:T(8,128)S(1)}, f32[98,8,128]{2,1,0:T(8,128)S(1)}, u32[]{:S(2)}, u32[]{:S(2)}) %collective-permute-start) | collective-permute-done | bytes 401440 | tf_op jit(solution)/shard_map/ppermute | solution.py:277
  5.0 1.4 %pack.1 = (f32[64,24,128]{2,1,0:T(8,128)}, f32[8,128]{1,0:T(8,128)S(1)}) custom-call(f32[96,8,128]{2,1,0:T(8,128)S(1)} %get-tuple-element.15.own_ref, f32[98,8,128]{2,1,0:T(8,128)S(1)} %collective-permute-done.got_ref, f32[3,8,128]{2,1,0:T(8,128)S(1)} %get-tuple-element.17.keep_ref), custom_call_target="tpu_custom_call" | custom-call | tf_op jit(solution)/shard_map/pack/pallas_call | solution.py:286
  6.4 11.2 %all-to-all-start = ((f32[64,24,128]{2,1,0:T(8,128)}), f32[64,24,128]{2,1,0:T(8,128)S(1)}, u32[]{:S(2)}, u32[]{:S(2)}) async-start(f32[64,24,128]{2,1,0:T(8,128)} %get-tuple-element.18), calls=%async_computation | async-start | bytes 1572864 | tf_op jit(solution)/shard_map/all_to_all | solution.py:294
  17.6 0.0 copy-start.1
  17.6 1.2 %copy-done.1 = f32[512,512]{1,0:T(8,128)S(1)} copy-done((f32[512,512]{1,0:T(8,128)S(1)}, f32[512,512]{1,0:T(8,128)}, u32[]{:S(2)}) %copy-start.1) | copy-done | bytes 1048600
  18.9 0.3 split.1.halves_ref
  19.2 13.6 %all-to-all-done.in_ref = f32[64,24,128]{2,1,0:T(8,128)S(1)} async-done(((f32[64,24,128]{2,1,0:T(8,128)}), f32[64,24,128]{2,1,0:T(8,128)S(1)}, u32[]{:S(2)}, u32[]{:S(2)}) %all-to-all-start) | async-done | bytes 786464 | tf_op jit(solution)/shard_map/all_to_all | solution.py:294
  32.8 0.0 copy-start
  32.8 0.0 copy-start.2
  32.8 5.1 %work.1 = f32[64,8,128]{2,1,0:T(8,128)S(1)} custom-call(f32[64,24,128]{2,1,0:T(8,128)S(1)} %all-to-all-done.in_ref, bf16[4,512,512]{2,1,0:T(8,128)(2,1)S(1)} %split.1.halves_ref, f32[8,128]{1,0:T(8,128)S(1)} %get-tuple-element.19.kept_ref), custom_call_target="tpu_custom_call" | custom-call | tf_op jit(solution)/shard_map/work/pallas_call | solution.py:296
  37.9 13.9 %all_to_all.10.back_ref = f32[64,8,128]{2,1,0:T(8,128)S(1)} all-to-all(f32[64,8,128]{2,1,0:T(8,128)S(1)} %work.1), channel_id=1, replica_groups=mesh['ocean'=2,'ice'=64] {'ice'}, dimensions={0} | all-to-all | bytes 524288 | tf_op jit(solution)/shard_map/all_to_all | solution.py:310
  51.8 3.0 %collective-permute-start.1 = (f32[64,8,128]{2,1,0:T(8,128)S(1)}, f32[64,8,128]{2,1,0:T(8,128)S(1)}, u32[]{:S(2)}, u32[]{:S(2)}) collective-permute-start(f32[64,8,128]{2,1,0:T(8,128)S(1)} %all_to_all.10.back_ref), channel_id=1, source_target_pairs={{0,64},{64,0},{1,65},{65,1},{2,66},{66,2},{3,67},{67,3},{4,68},{68... | collective-permute-start | bytes 786440 | tf_op jit(solution)/shard_map/ppermute | solution.py:311
  54.8 0.0 copy-done
  54.8 0.0 copy-done.2
  54.8 1.5 %near.1 = (f32[4,65,8,128]{3,2,1,0:T(8,128)S(1)}, s32[32]{0:T(128)S(1)}) custom-call(s32[64]{0:T(128)S(1)} %copy-done.2, f32[64,8,128]{2,1,0:T(8,128)S(1)} %all_to_all.10.back_ref, s32[64,8,128]{2,1,0:T(8,128)S(1)} %copy-done), custom_call_target="tpu_custom_call" | custom-call | tf_op jit(solution)/shard_map/near/pallas_call | solution.py:312
  56.4 0.0 collective-permute-done.1.far_ref
  56.4 1.7 %far.1 = (f32[64,8,128]{2,1,0:T(8,128)}, f32[64,8,128]{2,1,0:T(8,128)}, f32[64,8,128]{2,1,0:T(8,128)}, f32[64,8,128]{2,1,0:T(8,128)}, f32[4,65,8,128]{3,2,1,0:T(8,128)S(1)}) custom-call(s32[32]{0:T(128)S(1)} %get-tuple-element.20.index_ref, f32[64,8,128]{2,1,0:T(8,128)S(1)} %collective-permute-done.1.far_ref, ...), custom_call_target="tpu_custom_call", output_to_operand_aliasing={{4}: (3, {})} | custom-call | tf_op jit(solution)/shard_map/far/pallas_call | solution.py:320
Async XLA Ops:
  2.2 2.9 %collective-permute-start = (f32[98,8,128]{2,1,0:T(8,128)S(1)}, f32[98,8,128]{2,1,0:T(8,128)S(1)}, u32[]{:S(2)}, u32[]{:S(2)}) collective-permute-start(f32[98,8,128]{2,1,0:T(8,128)S(1)} %get-tuple-element.16), channel_id=1, source_target_pairs={{0,64},{64,0},{1,65},{65,1},{2,66},{66,2},{3,67},{67,3},{4,68},{68... | collective-permute-start | bytes 1204232 | tf_op jit(solution)/shard_map/ppermute | solution.py:277
  6.4 26.4 %all-to-all-start = ((f32[64,24,128]{2,1,0:T(8,128)}), f32[64,24,128]{2,1,0:T(8,128)S(1)}, u32[]{:S(2)}, u32[]{:S(2)}) async-start(f32[64,24,128]{2,1,0:T(8,128)} %get-tuple-element.18), calls=%async_computation | async-start | bytes 1572864 | tf_op jit(solution)/shard_map/all_to_all | solution.py:294
  17.6 1.2 %copy-start.1 = (f32[512,512]{1,0:T(8,128)S(1)}, f32[512,512]{1,0:T(8,128)}, u32[]{:S(2)}) copy-start(f32[512,512]{1,0:T(8,128)} %kernel_ref.1) | copy-start | bytes 3145732
  32.8 22.0 %copy-start = (s32[64,8,128]{2,1,0:T(8,128)S(1)}, s32[64,8,128]{2,1,0:T(8,128)}, u32[]{:S(2)}) copy-start(s32[64,8,128]{2,1,0:T(8,128)} %switch_ref.3) | copy-start | bytes 786436
  32.8 22.0 %copy-start.2 = (s32[64]{0:T(128)S(1)}, s32[64]{0:T(128)}, u32[]{:S(2)}) copy-start(s32[64]{0:T(128)} %covered_ref.1) | copy-start | bytes 772
  51.8 4.6 %collective-permute-start.1 = (f32[64,8,128]{2,1,0:T(8,128)S(1)}, f32[64,8,128]{2,1,0:T(8,128)S(1)}, u32[]{:S(2)}, u32[]{:S(2)}) collective-permute-start(f32[64,8,128]{2,1,0:T(8,128)S(1)} %all_to_all.10.back_ref), channel_id=1, source_target_pairs={{0,64},{64,0},{1,65},{65,1},{2,66},{66,2},{3,67},{67,3},{4,68},{68... | collective-permute-start | bytes 786440 | tf_op jit(solution)/shard_map/ppermute | solution.py:311

commit v7 on v6

--- a/solution.py
+++ b/solution.py
@@ -88,12 +88,13 @@
     halves_ref[2], halves_ref[3] = split(whole.T)
 
 
-def pack_kernel(own_ref, got_ref, keep_ref, out_ref, kept_ref):
+def pack_kernel(own_ref, got_ref, keep_ref, packed_hbm, kept_ref, out_ref, sems):
     heavy = keep_ref[2] > 0.5
     lane = lax.broadcasted_iota(jnp.int32, (8, 128), 1)
     low = lane < 64
     spot = lane % 64
 
+    copies = []
     for k in range(SLOTS):
         tiles = [own_ref[6 * k + f] for f in range(6)]
         if k < SLOTS - 1:
@@ -111,12 +112,18 @@
                 if q == PARTS - 1:
                     both = jnp.where(spot < 48, both, 0.0)
                 out_ref[PARTS * k + q, pl.ds(8 * t, 8), :] = both
+        if k % 4 == 3:
+            rows = pl.ds(PARTS * (k - 3), 4 * PARTS)
+            copies.append(pltpu.make_async_copy(out_ref.at[rows], packed_hbm.at[rows], sems.at[k // 4]))
+            copies[-1].start()
     slot = lax.axis_index("ice") // PARTS
     sub = slot % 8
     mine = jnp.broadcast_to(keep_ref[slot // 8, pl.ds(sub, 1), :], (8, 128))
     other = jnp.broadcast_to(got_ref[6 * SLOTS + slot // 8, pl.ds(sub, 1), :], (8, 128))
     own_slot = jnp.full((8, 128), slot, jnp.int32) == SLOTS - 1
     kept_ref[...] = jnp.where(jnp.logical_or(heavy, own_slot), mine, other)
+    for copy in copies:
+        copy.wait()
 
 
 def product(a_high, a_low, b):
@@ -203,28 +210,29 @@
         total = acc_ref[v]
         col_ref[spread(v), :] = total + pltpu.roll(total, 64, 1)
     adj_q = product(halves_ref[2], halves_ref[3], col_ref[...])
+    turn = [lax.rem(32 * (f + part) + 48, 128) for f in range(4)]
+    field = lax.rem(lane // 32 + (PARTS - part), PARTS)
     for v in range(GROUPS):
         tile = jnp.where(
-            lane < 32,
-            pltpu.roll(x_ref[v], 48, 1),
-            jnp.where(lane < 64, GAMMA * pltpu.roll(y_ref[v], 80, 1), STEP * pltpu.roll(af_ref[v], 16, 1)),
+            field == 0,
+            pltpu.roll(x_ref[v], turn[0], 1),
+            jnp.where(
+                field == 1, GAMMA * pltpu.roll(y_ref[v], turn[1], 1), STEP * pltpu.roll(af_ref[v], turn[3], 1)
+            ),
         )
         col_ref[spread(v), :] = tile
-    here = jnp.logical_and(lane >= 64, lane < 96)[None]
-    moved = pltpu.roll(adj_q, 48, 1).reshape(GROUPS, 8, 128)
-    result = jnp.where(here, moved, col_ref[...].reshape(GROUPS, 8, 128))
+    moved = pltpu.roll(adj_q, turn[2], 1).reshape(GROUPS, 8, 128)
+    result = jnp.where((field == 2)[None], moved, col_ref[...].reshape(GROUPS, 8, 128))
     out_ref[...] = result
 
 
 def unpack(back_ref, switch_ref, all_ref, f, base, block):
     lane = lax.broadcasted_iota(jnp.int32, (8, 128), 1)
-    whole = None
-    for q in range(PARTS):
-        shift = (32 * (q - f)) % 128
-        moved = back_ref[base + q]
-        if shift:
-            moved = pltpu.roll(moved, shift, 1)
-        whole = moved if q == 0 else jnp.where(lane >= 32 * q, moved, whole)
+    whole = back_ref[base + (-f) % PARTS]
+    for g in range(1, PARTS):
+        whole = jnp.where(lane >= 32 * g, back_ref[base + (g - f) % PARTS], whole)
+    if f:
+        whole = pltpu.roll(whole, 128 - 32 * f, 1)
     if f == 2:
         inside = jnp.minimum(block, BLOCKS - 1)
         whole = whole * jnp.where(switch_ref[inside] == 1, PLASTIC, VISCOUS)
@@ -288,7 +296,8 @@
         name="pack",
         out_shape=(jax.ShapeDtypeStruct((ICE, 24, 128), F32), sds()),
         in_specs=[vmem()] * 3,
-        out_specs=(vmem(), vmem()),
+        out_specs=(pl.BlockSpec(memory_space=pltpu.HBM), vmem()),
+        scratch_shapes=[pltpu.VMEM((ICE, 24, 128), F32), pltpu.SemaphoreType.DMA((4,))],
         compiler_params=params,
     )(own, got, keep)
     arrived = lax.all_to_all(packed, "ice", split_axis=0, concat_axis=0, tiled=True)

time: 58.3 us -> 58 us (level)
  no operation moved by 1% of the time
where the time goes in v7:
time: 58 us; the launch traced here: 57.7 us
  starting transfers between devices  15.8 us (27%)
  waiting for transfers between devices  15 us (26%)
  blocking collectives  13.9 us (24%)
  Pallas kernels  11.1 us (19%)
  local copies, waits for them, and re-layouts  1.23 us (2%)
  between operations  0.7 us (1%)
    all_to_all x1, blocking collectives, shards(): lax.all_to_all(result, 'ice', split_axis=0, concat_axis=0, tiled=True)  13.9 us
    all_to_all x1, waiting for transfers between devices, shards(): lax.all_to_all(packed, 'ice', split_axis=0, concat_axis=0, tiled=True)  13.6 us
    all_to_all x1, starting transfers between devices, shards(): lax.all_to_all(packed, 'ice', split_axis=0, concat_axis=0, tiled=True)  11.2 us
    pallas_call x1, Pallas kernels, shards(): pl.pallas_call(work_kernel, name='work', out_shape=sds(ICE), in_specs=[vm...  5.07 us
    ppermute x1, starting transfers between devices, shards(): far = lax.ppermute(back, 'ocean', [(0, 1), (1, 0)])  3.05 us
    pallas_call x1, Pallas kernels, shards(): pl.pallas_call(far_kernel, name='far', out_shape=(sds(BLOCKS),) * 4 + (sd...  1.57 us
    pallas_call x1, Pallas kernels, shards(): pl.pallas_call(gather_kernel, name='gather', out_shape=(sds(6 * SLOTS), s...  1.54 us
    ppermute x1, starting transfers between devices, shards(): got = lax.ppermute(send, 'ocean', [(0, 1), (1, 0)])  1.5 us
  transfers between devices with their start and end apart: 3, of which 2 were waited for; matrix products, arithmetic and copies ran while one was open for 0% of the time, Pallas kernels for 3%

profile of v7, /device:TPU:1, one launch (start us, length us, event | category | flops | bytes accessed | tf_op | source)
XLA Modules:
  0.0 57.7 jit_solution(750621952965730128)
XLA Ops:
  0.6 1.5 %gather.1 = (f32[96,8,128]{2,1,0:T(8,128)S(1)}, f32[98,8,128]{2,1,0:T(8,128)S(1)}, f32[3,8,128]{2,1,0:T(8,128)S(1)}) custom-call(s32[64]{0:T(128)} %covered_ref.1, s32[64]{0:T(128)} %reinit_hbm.1, f32[64,8,128]{2,1,0:T(8,128)} %velo_hbm.1, f32[64,8,128]{2,1,0:T(8,128)} %cotu_hbm.1, f32[64,8,128]{2,1,0:T(8,128)} %stress_hbm.1, f32[64,8,128]{2,1,0:T(8,128)} %cots_hbm.1, ...), custom_call_target="tpu_custom_call" | custom-call | tf_op jit(solution)/shard_map/gather/pallas_call | solution.py:271
  2.2 1.5 %collective-permute-start = (f32[98,8,128]{2,1,0:T(8,128)S(1)}, f32[98,8,128]{2,1,0:T(8,128)S(1)}, u32[]{:S(2)}, u32[]{:S(2)}) collective-permute-start(f32[98,8,128]{2,1,0:T(8,128)S(1)} %get-tuple-element.16), channel_id=1, source_target_pairs={{0,64},{64,0},{1,65},{65,1},{2,66},{66,2},{3,67},{67,3},{4,68},{68... | collective-permute-start | bytes 1204232 | tf_op jit(solution)/shard_map/ppermute | solution.py:285
  3.7 1.4 %collective-permute-done.got_ref = f32[98,8,128]{2,1,0:T(8,128)S(1)} collective-permute-done((f32[98,8,128]{2,1,0:T(8,128)S(1)}, f32[98,8,128]{2,1,0:T(8,128)S(1)}, u32[]{:S(2)}, u32[]{:S(2)}) %collective-permute-start) | collective-permute-done | bytes 401440 | tf_op jit(solution)/shard_map/ppermute | solution.py:285
  5.0 1.2 %pack.1 = (f32[64,24,128]{2,1,0:T(8,128)}, f32[8,128]{1,0:T(8,128)S(1)}) custom-call(f32[96,8,128]{2,1,0:T(8,128)S(1)} %get-tuple-element.15.own_ref, f32[98,8,128]{2,1,0:T(8,128)S(1)} %collective-permute-done.got_ref, f32[3,8,128]{2,1,0:T(8,128)S(1)} %get-tuple-element.17.keep_ref), custom_call_target="tpu_custom_call" | custom-call | tf_op jit(solution)/shard_map/pack/pallas_call | solution.py:294
  6.2 11.2 %all-to-all-start = ((f32[64,24,128]{2,1,0:T(8,128)}), f32[64,24,128]{2,1,0:T(8,128)S(1)}, u32[]{:S(2)}, u32[]{:S(2)}) async-start(f32[64,24,128]{2,1,0:T(8,128)} %get-tuple-element.18), calls=%async_computation | async-start | bytes 1572864 | tf_op jit(solution)/shard_map/all_to_all | solution.py:303
  17.5 0.0 copy-start.1
  17.5 1.2 %copy-done.1 = f32[512,512]{1,0:T(8,128)S(1)} copy-done((f32[512,512]{1,0:T(8,128)S(1)}, f32[512,512]{1,0:T(8,128)}, u32[]{:S(2)}) %copy-start.1) | copy-done | bytes 1048600
  18.7 0.3 split.1.halves_ref
  19.1 13.6 %all-to-all-done.in_ref = f32[64,24,128]{2,1,0:T(8,128)S(1)} async-done(((f32[64,24,128]{2,1,0:T(8,128)}), f32[64,24,128]{2,1,0:T(8,128)S(1)}, u32[]{:S(2)}, u32[]{:S(2)}) %all-to-all-start) | async-done | bytes 786464 | tf_op jit(solution)/shard_map/all_to_all | solution.py:303
  32.7 0.0 copy-start
  32.7 0.0 copy-start.2
  32.7 5.1 %work.1 = f32[64,8,128]{2,1,0:T(8,128)S(1)} custom-call(f32[64,24,128]{2,1,0:T(8,128)S(1)} %all-to-all-done.in_ref, bf16[4,512,512]{2,1,0:T(8,128)(2,1)S(1)} %split.1.halves_ref, f32[8,128]{1,0:T(8,128)S(1)} %get-tuple-element.19.kept_ref), custom_call_target="tpu_custom_call" | custom-call | tf_op jit(solution)/shard_map/work/pallas_call | solution.py:305
  37.7 13.9 %all_to_all.10.back_ref = f32[64,8,128]{2,1,0:T(8,128)S(1)} all-to-all(f32[64,8,128]{2,1,0:T(8,128)S(1)} %work.1), channel_id=1, replica_groups=mesh['ocean'=2,'ice'=64] {'ice'}, dimensions={0} | all-to-all | bytes 524288 | tf_op jit(solution)/shard_map/all_to_all | solution.py:319
  51.6 3.0 %collective-permute-start.1 = (f32[64,8,128]{2,1,0:T(8,128)S(1)}, f32[64,8,128]{2,1,0:T(8,128)S(1)}, u32[]{:S(2)}, u32[]{:S(2)}) collective-permute-start(f32[64,8,128]{2,1,0:T(8,128)S(1)} %all_to_all.10.back_ref), channel_id=1, source_target_pairs={{0,64},{64,0},{1,65},{65,1},{2,66},{66,2},{3,67},{67,3},{4,68},{68... | collective-permute-start | bytes 786440 | tf_op jit(solution)/shard_map/ppermute | solution.py:320
  54.7 0.0 copy-done
  54.7 0.0 copy-done.2
  54.7 1.4 %near.1 = (f32[4,65,8,128]{3,2,1,0:T(8,128)S(1)}, s32[32]{0:T(128)S(1)}) custom-call(s32[64]{0:T(128)S(1)} %copy-done.2, f32[64,8,128]{2,1,0:T(8,128)S(1)} %all_to_all.10.back_ref, s32[64,8,128]{2,1,0:T(8,128)S(1)} %copy-done), custom_call_target="tpu_custom_call" | custom-call | tf_op jit(solution)/shard_map/near/pallas_call | solution.py:321
  56.1 0.0 collective-permute-done.1.far_ref
  56.1 1.6 %far.1 = (f32[64,8,128]{2,1,0:T(8,128)}, f32[64,8,128]{2,1,0:T(8,128)}, f32[64,8,128]{2,1,0:T(8,128)}, f32[64,8,128]{2,1,0:T(8,128)}, f32[4,65,8,128]{3,2,1,0:T(8,128)S(1)}) custom-call(s32[32]{0:T(128)S(1)} %get-tuple-element.20.index_ref, f32[64,8,128]{2,1,0:T(8,128)S(1)} %collective-permute-done.1.far_ref, ...), custom_call_target="tpu_custom_call", output_to_operand_aliasing={{4}: (3, {})} | custom-call | tf_op jit(solution)/shard_map/far/pallas_call | solution.py:329
Async XLA Ops:
  2.2 2.9 %collective-permute-start = (f32[98,8,128]{2,1,0:T(8,128)S(1)}, f32[98,8,128]{2,1,0:T(8,128)S(1)}, u32[]{:S(2)}, u32[]{:S(2)}) collective-permute-start(f32[98,8,128]{2,1,0:T(8,128)S(1)} %get-tuple-element.16), channel_id=1, source_target_pairs={{0,64},{64,0},{1,65},{65,1},{2,66},{66,2},{3,67},{67,3},{4,68},{68... | collective-permute-start | bytes 1204232 | tf_op jit(solution)/shard_map/ppermute | solution.py:285
  6.2 26.4 %all-to-all-start = ((f32[64,24,128]{2,1,0:T(8,128)}), f32[64,24,128]{2,1,0:T(8,128)S(1)}, u32[]{:S(2)}, u32[]{:S(2)}) async-start(f32[64,24,128]{2,1,0:T(8,128)} %get-tuple-element.18), calls=%async_computation | async-start | bytes 1572864 | tf_op jit(solution)/shard_map/all_to_all | solution.py:303
  17.5 1.2 %copy-start.1 = (f32[512,512]{1,0:T(8,128)S(1)}, f32[512,512]{1,0:T(8,128)}, u32[]{:S(2)}) copy-start(f32[512,512]{1,0:T(8,128)} %kernel_ref.1) | copy-start | bytes 3145732
  32.7 22.0 %copy-start = (s32[64,8,128]{2,1,0:T(8,128)S(1)}, s32[64,8,128]{2,1,0:T(8,128)}, u32[]{:S(2)}) copy-start(s32[64,8,128]{2,1,0:T(8,128)} %switch_ref.3) | copy-start | bytes 786436
  32.7 22.0 %copy-start.2 = (s32[64]{0:T(128)S(1)}, s32[64]{0:T(128)}, u32[]{:S(2)}) copy-start(s32[64]{0:T(128)} %covered_ref.1) | copy-start | bytes 772
  51.6 4.4 %collective-permute-start.1 = (f32[64,8,128]{2,1,0:T(8,128)S(1)}, f32[64,8,128]{2,1,0:T(8,128)S(1)}, u32[]{:S(2)}, u32[]{:S(2)}) collective-permute-start(f32[64,8,128]{2,1,0:T(8,128)S(1)} %all_to_all.10.back_ref), channel_id=1, source_target_pairs={{0,64},{64,0},{1,65},{65,1},{2,66},{66,2},{3,67},{67,3},{4,68},{68... | collective-permute-start | bytes 786440 | tf_op jit(solution)/shard_map/ppermute | solution.py:320

commit v8 on v7

--- a/solution.py
+++ b/solution.py
@@ -88,42 +88,50 @@
     halves_ref[2], halves_ref[3] = split(whole.T)
 
 
-def pack_kernel(own_ref, got_ref, keep_ref, packed_hbm, kept_ref, out_ref, sems):
-    heavy = keep_ref[2] > 0.5
+def pack(fields_ref, slots, packed_hbm, out_ref, sems):
     lane = lax.broadcasted_iota(jnp.int32, (8, 128), 1)
     low = lane < 64
     spot = lane % 64
-
     copies = []
-    for k in range(SLOTS):
-        tiles = [own_ref[6 * k + f] for f in range(6)]
-        if k < SLOTS - 1:
-            tiles = [jnp.where(heavy, tile, got_ref[6 * k + f]) for f, tile in enumerate(tiles)]
+    sent = 0
+    for k in range(slots):
+        tiles = [fields_ref[6 * k + f] for f in range(6)]
         for q in range(PARTS):
             shift = (16 - 32 * q) % 128
             for t in range(3):
                 both = jnp.where(
-                    low,
-                    pltpu.roll(tiles[2 * t], shift, 1) if shift else tiles[2 * t],
-                    pltpu.roll(tiles[2 * t + 1], (shift + 64) % 128, 1),
+                    low, pltpu.roll(tiles[2 * t], shift, 1), pltpu.roll(tiles[2 * t + 1], (shift + 64) % 128, 1)
                 )
                 if q == 0:
                     both = jnp.where(spot >= 16, both, 0.0)
                 if q == PARTS - 1:
                     both = jnp.where(spot < 48, both, 0.0)
                 out_ref[PARTS * k + q, pl.ds(8 * t, 8), :] = both
-        if k % 4 == 3:
-            rows = pl.ds(PARTS * (k - 3), 4 * PARTS)
+        if k % 4 == 3 or k == slots - 1:
+            rows = pl.ds(PARTS * sent, PARTS * (k + 1 - sent))
             copies.append(pltpu.make_async_copy(out_ref.at[rows], packed_hbm.at[rows], sems.at[k // 4]))
             copies[-1].start()
+            sent = k + 1
+    for copy in copies:
+        copy.wait()
+
+
+def pack_own_kernel(own_ref, packed_hbm, out_ref, sems):
+    pack(own_ref, SLOTS, packed_hbm, out_ref, sems)
+
+
+def pack_got_kernel(got_ref, keep_ref, own_hbm, packed_hbm, kept_ref, out_ref, sems):
+    heavy = keep_ref[2] > 0.5
     slot = lax.axis_index("ice") // PARTS
     sub = slot % 8
     mine = jnp.broadcast_to(keep_ref[slot // 8, pl.ds(sub, 1), :], (8, 128))
     other = jnp.broadcast_to(got_ref[6 * SLOTS + slot // 8, pl.ds(sub, 1), :], (8, 128))
     own_slot = jnp.full((8, 128), slot, jnp.int32) == SLOTS - 1
     kept_ref[...] = jnp.where(jnp.logical_or(heavy, own_slot), mine, other)
-    for copy in copies:
-        copy.wait()
+
+    @pl.when(jnp.max(keep_ref[2]) < 0.5)
+    def light():
+        pack(got_ref, SLOTS - 1, packed_hbm, out_ref, sems)
 
 
 def product(a_high, a_low, b):
@@ -291,15 +299,28 @@
         out_specs=vmem(),
         compiler_params=params,
     )(kernel)
+    windows = jax.ShapeDtypeStruct((ICE, 24, 128), F32)
+    hbm = pl.BlockSpec(memory_space=pltpu.HBM)
+    staging = [pltpu.VMEM((ICE, 24, 128), F32), pltpu.SemaphoreType.DMA((4,))]
+    packed = pl.pallas_call(
+        pack_own_kernel,
+        name="pack_own",
+        out_shape=windows,
+        in_specs=[vmem()],
+        out_specs=hbm,
+        scratch_shapes=staging,
+        compiler_params=params,
+    )(own)
     packed, kept = pl.pallas_call(
-        pack_kernel,
-        name="pack",
-        out_shape=(jax.ShapeDtypeStruct((ICE, 24, 128), F32), sds()),
-        in_specs=[vmem()] * 3,
-        out_specs=(pl.BlockSpec(memory_space=pltpu.HBM), vmem()),
-        scratch_shapes=[pltpu.VMEM((ICE, 24, 128), F32), pltpu.SemaphoreType.DMA((4,))],
-        compiler_params=params,
-    )(own, got, keep)
+        pack_got_kernel,
+        name="pack_got",
+        out_shape=(windows, sds()),
+        in_specs=[vmem(), vmem(), hbm],
+        out_specs=(hbm, vmem()),
+        scratch_shapes=staging,
+        input_output_aliases={2: 0},
+        compiler_params=params,
+    )(got, keep, packed)
     arrived = lax.all_to_all(packed, "ice", split_axis=0, concat_axis=0, tiled=True)
     col = pltpu.VMEM((GROUPS,) + tile, F32)
     result = pl.pallas_call(

time: 58 us -> 56.9 us (0.981)
  waiting for transfers between devices: 15 us -> 12.7 us
  starting transfers between devices: 15.8 us -> 16.9 us
    ppermute x1, waiting for transfers between devices: 1.36 us -> 0.18 us  [shards(): got = lax.ppermute(send, 'ocean', [(0, 1), (1, 0)])]
    ppermute x1, starting transfers between devices: 3.05 us -> 4.2 us  [shards(): far = lax.ppermute(back, 'ocean', [(0, 1), (1, 0)])]
    all_to_all x1, waiting for transfers between devices: 13.6 us -> 12.5 us  [shards(): lax.all_to_all(packed, 'ice', split_axis=0, concat_axis=0, tiled=True)]
    pallas_call x1 -> x2, Pallas kernels: 1.19 us -> 1.33 us  [the longest x1 1.18 us: shards(): pl.pallas_call(pack_own_kernel, name='pack_own', out_shape=windows, in_sp...]
  transfers between devices with their start and end apart: 3 -> 3, of which waited for: 2 -> 2; matrix products, arithmetic and copies ran while one was open for 0% -> 0% of each run, Pallas kernels for 3% -> 5%
where the time goes in v8:
time: 56.9 us; the launch traced here: 56.6 us
  starting transfers between devices  16.9 us (30%)
  blocking collectives  13.8 us (24%)
  waiting for transfers between devices  12.7 us (22%)
  Pallas kernels  11.2 us (20%)
  local copies, waits for them, and re-layouts  1.23 us (2%)
  between operations  0.7 us (1%)
    all_to_all x1, blocking collectives, shards(): lax.all_to_all(result, 'ice', split_axis=0, concat_axis=0, tiled=True)  13.8 us
    all_to_all x1, waiting for transfers between devices, shards(): lax.all_to_all(packed, 'ice', split_axis=0, concat_axis=0, tiled=True)  12.5 us
    all_to_all x1, starting transfers between devices, shards(): lax.all_to_all(packed, 'ice', split_axis=0, concat_axis=0, tiled=True)  11.2 us
    pallas_call x1, Pallas kernels, shards(): pl.pallas_call(work_kernel, name='work', out_shape=sds(ICE), in_specs=[vm...  5.07 us
    ppermute x1, starting transfers between devices, shards(): far = lax.ppermute(back, 'ocean', [(0, 1), (1, 0)])  4.2 us
    pallas_call x1, Pallas kernels, shards(): pl.pallas_call(far_kernel, name='far', out_shape=(sds(BLOCKS),) * 4 + (sd...  1.57 us
    pallas_call x1, Pallas kernels, shards(): pl.pallas_call(gather_kernel, name='gather', out_shape=(sds(6 * SLOTS), s...  1.54 us
    ppermute x1, starting transfers between devices, shards(): got = lax.ppermute(send, 'ocean', [(0, 1), (1, 0)])  1.5 us
  transfers between devices with their start and end apart: 3, of which 2 were waited for; matrix products, arithmetic and copies ran while one was open for 0% of the time, Pallas kernels for 5%

profile of v8, /device:TPU:1, one launch (start us, length us, event | category | flops | bytes accessed | tf_op | source)
XLA Modules:
  0.0 56.6 jit_solution(8247931465023088760)
XLA Ops:
  0.6 1.5 %gather.1 = (f32[96,8,128]{2,1,0:T(8,128)S(1)}, f32[98,8,128]{2,1,0:T(8,128)S(1)}, f32[3,8,128]{2,1,0:T(8,128)S(1)}) custom-call(s32[64]{0:T(128)} %covered_ref.1, s32[64]{0:T(128)} %reinit_hbm.1, f32[64,8,128]{2,1,0:T(8,128)} %velo_hbm.1, f32[64,8,128]{2,1,0:T(8,128)} %cotu_hbm.1, f32[64,8,128]{2,1,0:T(8,128)} %stress_hbm.1, f32[64,8,128]{2,1,0:T(8,128)} %cots_hbm.1, ...), custom_call_target="tpu_custom_call" | custom-call | tf_op jit(solution)/shard_map/gather/pallas_call | solution.py:279
  2.2 1.5 %collective-permute-start = (f32[98,8,128]{2,1,0:T(8,128)S(1)}, f32[98,8,128]{2,1,0:T(8,128)S(1)}, u32[]{:S(2)}, u32[]{:S(2)}) collective-permute-start(f32[98,8,128]{2,1,0:T(8,128)S(1)} %get-tuple-element.15), channel_id=1, source_target_pairs={{0,64},{64,0},{1,65},{65,1},{2,66},{66,2},{3,67},{67,3},{4,68},{68... | collective-permute-start | bytes 1204232 | tf_op jit(solution)/shard_map/ppermute | solution.py:293
  3.7 1.2 %pack_own.1.own_hbm = f32[64,24,128]{2,1,0:T(8,128)} custom-call(f32[96,8,128]{2,1,0:T(8,128)S(1)} %get-tuple-element.17.own_ref), custom_call_target="tpu_custom_call" | custom-call | tf_op jit(solution)/shard_map/pack_own/pallas_call | solution.py:305
  4.9 0.2 collective-permute-done.got_ref
  5.0 0.2 pack_got.1
  5.2 11.2 %all-to-all-start = ((f32[64,24,128]{2,1,0:T(8,128)}), f32[64,24,128]{2,1,0:T(8,128)S(1)}, u32[]{:S(2)}, u32[]{:S(2)}) async-start(f32[64,24,128]{2,1,0:T(8,128)} %get-tuple-element.18), calls=%async_computation | async-start | bytes 1572864 | tf_op jit(solution)/shard_map/all_to_all | solution.py:324
  16.4 0.0 copy-start.1
  16.5 1.2 %copy-done.1 = f32[512,512]{1,0:T(8,128)S(1)} copy-done((f32[512,512]{1,0:T(8,128)S(1)}, f32[512,512]{1,0:T(8,128)}, u32[]{:S(2)}) %copy-start.1) | copy-done | bytes 1048600
  17.7 0.3 split.1.halves_ref
  18.0 12.5 %all-to-all-done.in_ref = f32[64,24,128]{2,1,0:T(8,128)S(1)} async-done(((f32[64,24,128]{2,1,0:T(8,128)}), f32[64,24,128]{2,1,0:T(8,128)S(1)}, u32[]{:S(2)}, u32[]{:S(2)}) %all-to-all-start) | async-done | bytes 786464 | tf_op jit(solution)/shard_map/all_to_all | solution.py:324
  30.6 0.0 copy-start
  30.6 0.0 copy-start.2
  30.6 5.1 %work.1 = f32[64,8,128]{2,1,0:T(8,128)S(1)} custom-call(f32[64,24,128]{2,1,0:T(8,128)S(1)} %all-to-all-done.in_ref, bf16[4,512,512]{2,1,0:T(8,128)(2,1)S(1)} %split.1.halves_ref, f32[8,128]{1,0:T(8,128)S(1)} %get-tuple-element.19.kept_ref), custom_call_target="tpu_custom_call" | custom-call | tf_op jit(solution)/shard_map/work/pallas_call | solution.py:326
  35.7 13.8 %all_to_all.10.back_ref = f32[64,8,128]{2,1,0:T(8,128)S(1)} all-to-all(f32[64,8,128]{2,1,0:T(8,128)S(1)} %work.1), channel_id=1, replica_groups=mesh['ocean'=2,'ice'=64] {'ice'}, dimensions={0} | all-to-all | bytes 524288 | tf_op jit(solution)/shard_map/all_to_all | solution.py:340
  49.5 4.2 %collective-permute-start.1 = (f32[64,8,128]{2,1,0:T(8,128)S(1)}, f32[64,8,128]{2,1,0:T(8,128)S(1)}, u32[]{:S(2)}, u32[]{:S(2)}) collective-permute-start(f32[64,8,128]{2,1,0:T(8,128)S(1)} %all_to_all.10.back_ref), channel_id=1, source_target_pairs={{0,64},{64,0},{1,65},{65,1},{2,66},{66,2},{3,67},{67,3},{4,68},{68... | collective-permute-start | bytes 786440 | tf_op jit(solution)/shard_map/ppermute | solution.py:341
  53.7 0.0 copy-done
  53.7 0.0 copy-done.2
  53.7 1.4 %near.1 = (f32[4,65,8,128]{3,2,1,0:T(8,128)S(1)}, s32[32]{0:T(128)S(1)}) custom-call(s32[64]{0:T(128)S(1)} %copy-done.2, f32[64,8,128]{2,1,0:T(8,128)S(1)} %all_to_all.10.back_ref, s32[64,8,128]{2,1,0:T(8,128)S(1)} %copy-done), custom_call_target="tpu_custom_call" | custom-call | tf_op jit(solution)/shard_map/near/pallas_call | solution.py:342
  55.0 0.0 collective-permute-done.1.far_ref
  55.1 1.6 %far.1 = (f32[64,8,128]{2,1,0:T(8,128)}, f32[64,8,128]{2,1,0:T(8,128)}, f32[64,8,128]{2,1,0:T(8,128)}, f32[64,8,128]{2,1,0:T(8,128)}, f32[4,65,8,128]{3,2,1,0:T(8,128)S(1)}) custom-call(s32[32]{0:T(128)S(1)} %get-tuple-element.20.index_ref, f32[64,8,128]{2,1,0:T(8,128)S(1)} %collective-permute-done.1.far_ref, ...), custom_call_target="tpu_custom_call", output_to_operand_aliasing={{4}: (3, {})} | custom-call | tf_op jit(solution)/shard_map/far/pallas_call | solution.py:350
Async XLA Ops:
  2.2 2.9 %collective-permute-start = (f32[98,8,128]{2,1,0:T(8,128)S(1)}, f32[98,8,128]{2,1,0:T(8,128)S(1)}, u32[]{:S(2)}, u32[]{:S(2)}) collective-permute-start(f32[98,8,128]{2,1,0:T(8,128)S(1)} %get-tuple-element.15), channel_id=1, source_target_pairs={{0,64},{64,0},{1,65},{65,1},{2,66},{66,2},{3,67},{67,3},{4,68},{68... | collective-permute-start | bytes 1204232 | tf_op jit(solution)/shard_map/ppermute | solution.py:293
  5.2 25.4 %all-to-all-start = ((f32[64,24,128]{2,1,0:T(8,128)}), f32[64,24,128]{2,1,0:T(8,128)S(1)}, u32[]{:S(2)}, u32[]{:S(2)}) async-start(f32[64,24,128]{2,1,0:T(8,128)} %get-tuple-element.18), calls=%async_computation | async-start | bytes 1572864 | tf_op jit(solution)/shard_map/all_to_all | solution.py:324
  16.4 1.2 %copy-start.1 = (f32[512,512]{1,0:T(8,128)S(1)}, f32[512,512]{1,0:T(8,128)}, u32[]{:S(2)}) copy-start(f32[512,512]{1,0:T(8,128)} %kernel_ref.1) | copy-start | bytes 3145732
  30.6 23.1 %copy-start = (s32[64,8,128]{2,1,0:T(8,128)S(1)}, s32[64,8,128]{2,1,0:T(8,128)}, u32[]{:S(2)}) copy-start(s32[64,8,128]{2,1,0:T(8,128)} %switch_ref.3) | copy-start | bytes 786436
  30.6 23.1 %copy-start.2 = (s32[64]{0:T(128)S(1)}, s32[64]{0:T(128)}, u32[]{:S(2)}) copy-start(s32[64]{0:T(128)} %covered_ref.1) | copy-start | bytes 772
  49.5 5.6 %collective-permute-start.1 = (f32[64,8,128]{2,1,0:T(8,128)S(1)}, f32[64,8,128]{2,1,0:T(8,128)S(1)}, u32[]{:S(2)}, u32[]{:S(2)}) collective-permute-start(f32[64,8,128]{2,1,0:T(8,128)S(1)} %all_to_all.10.back_ref), channel_id=1, source_target_pairs={{0,64},{64,0},{1,65},{65,1},{2,66},{66,2},{3,67},{67,3},{4,68},{68... | collective-permute-start | bytes 786440 | tf_op jit(solution)/shard_map/ppermute | solution.py:341

commit v9 on v8

--- a/solution.py
+++ b/solution.py
@@ -82,18 +82,10 @@
     return high, (x - high.astype(F32)).astype(BF16)
 
 
-def split_kernel(kernel_ref, halves_ref):
-    whole = kernel_ref[...]
-    halves_ref[0], halves_ref[1] = split(whole)
-    halves_ref[2], halves_ref[3] = split(whole.T)
-
-
-def pack(fields_ref, slots, packed_hbm, out_ref, sems):
+def pack(fields_ref, slots, out_ref):
     lane = lax.broadcasted_iota(jnp.int32, (8, 128), 1)
     low = lane < 64
     spot = lane % 64
-    copies = []
-    sent = 0
     for k in range(slots):
         tiles = [fields_ref[6 * k + f] for f in range(6)]
         for q in range(PARTS):
@@ -107,20 +99,19 @@
                 if q == PARTS - 1:
                     both = jnp.where(spot < 48, both, 0.0)
                 out_ref[PARTS * k + q, pl.ds(8 * t, 8), :] = both
-        if k % 4 == 3 or k == slots - 1:
-            rows = pl.ds(PARTS * sent, PARTS * (k + 1 - sent))
-            copies.append(pltpu.make_async_copy(out_ref.at[rows], packed_hbm.at[rows], sems.at[k // 4]))
-            copies[-1].start()
-            sent = k + 1
-    for copy in copies:
-        copy.wait()
-
-
-def pack_own_kernel(own_ref, packed_hbm, out_ref, sems):
-    pack(own_ref, SLOTS, packed_hbm, out_ref, sems)
-
-
-def pack_got_kernel(got_ref, keep_ref, own_hbm, packed_hbm, kept_ref, out_ref, sems):
+
+
+def pack_own_kernel(own_ref, kernel_hbm, out_ref, halves_ref, kernel_ref, sem):
+    copy = pltpu.make_async_copy(kernel_hbm, kernel_ref, sem)
+    copy.start()
+    pack(own_ref, SLOTS, out_ref)
+    copy.wait()
+    whole = kernel_ref[...]
+    halves_ref[0], halves_ref[1] = split(whole)
+    halves_ref[2], halves_ref[3] = split(whole.T)
+
+
+def pack_got_kernel(got_ref, keep_ref, packed_ref, out_ref, kept_ref):
     heavy = keep_ref[2] > 0.5
     slot = lax.axis_index("ice") // PARTS
     sub = slot % 8
@@ -131,7 +122,7 @@
 
     @pl.when(jnp.max(keep_ref[2]) < 0.5)
     def light():
-        pack(got_ref, SLOTS - 1, packed_hbm, out_ref, sems)
+        pack(got_ref, SLOTS - 1, out_ref)
 
 
 def product(a_high, a_low, b):
@@ -291,33 +282,22 @@
         for x in (covered, reinit, velocity, cot_velocity, stress, cot_stress, forcing, thickness, switch)
     ])
     got = lax.ppermute(send, "ocean", [(0, 1), (1, 0)])
-    halves = pl.pallas_call(
-        split_kernel,
-        name="split",
-        out_shape=jax.ShapeDtypeStruct((4, ROWS, ROWS), BF16),
-        in_specs=[vmem()],
-        out_specs=vmem(),
-        compiler_params=params,
-    )(kernel)
     windows = jax.ShapeDtypeStruct((ICE, 24, 128), F32)
-    hbm = pl.BlockSpec(memory_space=pltpu.HBM)
-    staging = [pltpu.VMEM((ICE, 24, 128), F32), pltpu.SemaphoreType.DMA((4,))]
-    packed = pl.pallas_call(
+    packed, halves = pl.pallas_call(
         pack_own_kernel,
         name="pack_own",
-        out_shape=windows,
-        in_specs=[vmem()],
-        out_specs=hbm,
-        scratch_shapes=staging,
-        compiler_params=params,
-    )(own)
+        out_shape=(windows, jax.ShapeDtypeStruct((4, ROWS, ROWS), BF16)),
+        in_specs=[vmem(), pl.BlockSpec(memory_space=pltpu.HBM)],
+        out_specs=(vmem(), vmem()),
+        scratch_shapes=[pltpu.VMEM((ROWS, ROWS), F32), pltpu.SemaphoreType.DMA],
+        compiler_params=params,
+    )(own, pltpu.with_memory_space_constraint(kernel, pltpu.HBM))
     packed, kept = pl.pallas_call(
         pack_got_kernel,
         name="pack_got",
         out_shape=(windows, sds()),
-        in_specs=[vmem(), vmem(), hbm],
-        out_specs=(hbm, vmem()),
-        scratch_shapes=staging,
+        in_specs=[vmem()] * 3,
+        out_specs=(vmem(), vmem()),
         input_output_aliases={2: 0},
         compiler_params=params,
     )(got, keep, packed)

time: 56.9 us -> 57.2 us (level)
  blocking collectives: 13.8 us -> 40.8 us
  starting transfers between devices: 16.9 us -> 3.72 us
  waiting for transfers between devices: 12.7 us -> 0.01 us
  local copies, waits for them, and re-layouts: 1.23 us -> 0.01 us
  Pallas kernels: 11.2 us -> 11.8 us
    all_to_all x0 -> x1, blocking collectives: none -> 26.9 us  [shards(): lax.all_to_all(packed, 'ice', split_axis=0, concat_axis=0, tiled=True)]
    all_to_all x1 -> x0, waiting for transfers between devices: 12.5 us -> none  [shards(): lax.all_to_all(packed, 'ice', split_axis=0, concat_axis=0, tiled=True)]
    all_to_all x1 -> x0, starting transfers between devices: 11.2 us -> none  [shards(): lax.all_to_all(packed, 'ice', split_axis=0, concat_axis=0, tiled=True)]
    ppermute x1, starting transfers between devices: 4.2 us -> 2.22 us  [shards(): far = lax.ppermute(back, 'ocean', [(0, 1), (1, 0)])]
    unnamed x6 -> x4, local copies, waits for them, and re-layouts: 1.23 us -> 0.01 us
    pallas_call x2 -> x1, Pallas kernels: 1.52 us -> 1.58 us  [shards(): pl.pallas_call(pack_own_kernel, name='pack_own', out_shape=(windows, jax....]
  transfers between devices with their start and end apart: 3 -> 2, of which waited for: 2 -> 0; matrix products, arithmetic and copies ran while one was open for 0% -> 0% of each run, Pallas kernels for 5% -> 5%
where the time goes in v9:
time: 57.2 us; the launch traced here: 57 us
  blocking collectives  40.8 us (71%)
  Pallas kernels  11.8 us (21%)
  starting transfers between devices  3.72 us (7%)
  between operations  0.69 us (1%)
    all_to_all x1, blocking collectives, shards(): lax.all_to_all(packed, 'ice', split_axis=0, concat_axis=0, tiled=True)  26.9 us
    all_to_all x1, blocking collectives, shards(): lax.all_to_all(result, 'ice', split_axis=0, concat_axis=0, tiled=True)  13.9 us
    pallas_call x1, Pallas kernels, shards(): pl.pallas_call(work_kernel, name='work', out_shape=sds(ICE), in_specs=[vm...  5.13 us
    ppermute x1, starting transfers between devices, shards(): far = lax.ppermute(back, 'ocean', [(0, 1), (1, 0)])  2.22 us
    pallas_call x1, Pallas kernels, shards(): pl.pallas_call(pack_own_kernel, name='pack_own', out_shape=(windows, jax....  1.58 us
    pallas_call x1, Pallas kernels, shards(): pl.pallas_call(far_kernel, name='far', out_shape=(sds(BLOCKS),) * 4 + (sd...  1.57 us
    pallas_call x1, Pallas kernels, shards(): pl.pallas_call(gather_kernel, name='gather', out_shape=(sds(6 * SLOTS), s...  1.54 us
    ppermute x1, starting transfers between devices, shards(): got = lax.ppermute(send, 'ocean', [(0, 1), (1, 0)])  1.5 us
  transfers between devices with their start and end apart: 2, of which 0 were waited for; matrix products, arithmetic and copies ran while one was open for 0% of the time, Pallas kernels for 5%

profile of v9, /device:TPU:1, one launch (start us, length us, event | category | flops | bytes accessed | tf_op | source)
XLA Modules:
  0.0 57.0 jit_solution(7589775000749588156)
XLA Ops:
  0.6 1.5 %gather.1 = (f32[96,8,128]{2,1,0:T(8,128)S(1)}, f32[98,8,128]{2,1,0:T(8,128)S(1)}, f32[3,8,128]{2,1,0:T(8,128)S(1)}) custom-call(s32[64]{0:T(128)} %covered_ref.1, s32[64]{0:T(128)} %reinit_hbm.1, f32[64,8,128]{2,1,0:T(8,128)} %velo_hbm.1, f32[64,8,128]{2,1,0:T(8,128)} %cotu_hbm.1, f32[64,8,128]{2,1,0:T(8,128)} %stress_hbm.1, f32[64,8,128]{2,1,0:T(8,128)} %cots_hbm.1, ...), custom_call_target="tpu_custom_call" | custom-call | tf_op jit(solution)/shard_map/gather/pallas_call | solution.py:270
  2.2 1.5 %collective-permute-start = (f32[98,8,128]{2,1,0:T(8,128)S(1)}, f32[98,8,128]{2,1,0:T(8,128)S(1)}, u32[]{:S(2)}, u32[]{:S(2)}) collective-permute-start(f32[98,8,128]{2,1,0:T(8,128)S(1)} %get-tuple-element.17), channel_id=1, source_target_pairs={{0,64},{64,0},{1,65},{65,1},{2,66},{66,2},{3,67},{67,3},{4,68},{68... | collective-permute-start | bytes 1204232 | tf_op jit(solution)/shard_map/ppermute | solution.py:284
  3.7 1.6 %pack_own.1 = (f32[64,24,128]{2,1,0:T(8,128)S(1)}, bf16[4,512,512]{2,1,0:T(8,128)(2,1)S(1)}) custom-call(f32[96,8,128]{2,1,0:T(8,128)S(1)} %get-tuple-element.19.own_ref, f32[512,512]{1,0:T(8,128)} %kernel_hbm.1), custom_call_target="tpu_custom_call" | custom-call | tf_op jit(solution)/shard_map/pack_own/pallas_call | solution.py:286
  5.3 0.0 collective-permute-done.got_ref
  5.3 0.6 pack_got.1
  5.8 26.9 %all_to_all.10.in_ref = f32[64,24,128]{2,1,0:T(8,128)S(1)} all-to-all(f32[64,24,128]{2,1,0:T(8,128)S(1)} %get-tuple-element.21), channel_id=1, replica_groups=mesh['ocean'=2,'ice'=64] {'ice'}, dimensions={0} | all-to-all | bytes 1572864 | tf_op jit(solution)/shard_map/all_to_all | solution.py:304
  32.8 0.0 copy-start
  32.8 0.0 copy-start.1
  32.8 5.1 %work.1 = f32[64,8,128]{2,1,0:T(8,128)S(1)} custom-call(f32[64,24,128]{2,1,0:T(8,128)S(1)} %all_to_all.10.in_ref, bf16[4,512,512]{2,1,0:T(8,128)(2,1)S(1)} %get-tuple-element.22.halves_ref, f32[8,128]{1,0:T(8,128)S(1)} %get-tuple-element.23.kept_ref), custom_call_target="tpu_custom_call" | custom-call | tf_op jit(solution)/shard_map/work/pallas_call | solution.py:306
  37.9 13.9 %all_to_all.11.back_ref = f32[64,8,128]{2,1,0:T(8,128)S(1)} all-to-all(f32[64,8,128]{2,1,0:T(8,128)S(1)} %work.1), channel_id=1, replica_groups=mesh['ocean'=2,'ice'=64] {'ice'}, dimensions={0} | all-to-all | bytes 524288 | tf_op jit(solution)/shard_map/all_to_all | solution.py:320
  51.8 2.2 %collective-permute-start.1 = (f32[64,8,128]{2,1,0:T(8,128)S(1)}, f32[64,8,128]{2,1,0:T(8,128)S(1)}, u32[]{:S(2)}, u32[]{:S(2)}) collective-permute-start(f32[64,8,128]{2,1,0:T(8,128)S(1)} %all_to_all.11.back_ref), channel_id=1, source_target_pairs={{0,64},{64,0},{1,65},{65,1},{2,66},{66,2},{3,67},{67,3},{4,68},{68... | collective-permute-start | bytes 786440 | tf_op jit(solution)/shard_map/ppermute | solution.py:321
  54.0 0.0 copy-done
  54.0 0.0 copy-done.1
  54.0 1.4 %near.1 = (f32[4,65,8,128]{3,2,1,0:T(8,128)S(1)}, s32[32]{0:T(128)S(1)}) custom-call(s32[64]{0:T(128)S(1)} %copy-done.1, f32[64,8,128]{2,1,0:T(8,128)S(1)} %all_to_all.11.back_ref, s32[64,8,128]{2,1,0:T(8,128)S(1)} %copy-done), custom_call_target="tpu_custom_call" | custom-call | tf_op jit(solution)/shard_map/near/pallas_call | solution.py:322
  55.4 0.0 collective-permute-done.1.far_ref
  55.4 1.6 %far.1 = (f32[64,8,128]{2,1,0:T(8,128)}, f32[64,8,128]{2,1,0:T(8,128)}, f32[64,8,128]{2,1,0:T(8,128)}, f32[64,8,128]{2,1,0:T(8,128)}, f32[4,65,8,128]{3,2,1,0:T(8,128)S(1)}) custom-call(s32[32]{0:T(128)S(1)} %get-tuple-element.24.index_ref, f32[64,8,128]{2,1,0:T(8,128)S(1)} %collective-permute-done.1.far_ref, ...), custom_call_target="tpu_custom_call", output_to_operand_aliasing={{4}: (3, {})} | custom-call | tf_op jit(solution)/shard_map/far/pallas_call | solution.py:330
Async XLA Ops:
  2.2 3.1 %collective-permute-start = (f32[98,8,128]{2,1,0:T(8,128)S(1)}, f32[98,8,128]{2,1,0:T(8,128)S(1)}, u32[]{:S(2)}, u32[]{:S(2)}) collective-permute-start(f32[98,8,128]{2,1,0:T(8,128)S(1)} %get-tuple-element.17), channel_id=1, source_target_pairs={{0,64},{64,0},{1,65},{65,1},{2,66},{66,2},{3,67},{67,3},{4,68},{68... | collective-permute-start | bytes 1204232 | tf_op jit(solution)/shard_map/ppermute | solution.py:284
  32.8 21.3 %copy-start = (s32[64,8,128]{2,1,0:T(8,128)S(1)}, s32[64,8,128]{2,1,0:T(8,128)}, u32[]{:S(2)}) copy-start(s32[64,8,128]{2,1,0:T(8,128)} %switch_ref.3) | copy-start | bytes 786436
  32.8 21.3 %copy-start.1 = (s32[64]{0:T(128)S(1)}, s32[64]{0:T(128)}, u32[]{:S(2)}) copy-start(s32[64]{0:T(128)} %covered_ref.1) | copy-start | bytes 772
  51.8 3.6 %collective-permute-start.1 = (f32[64,8,128]{2,1,0:T(8,128)S(1)}, f32[64,8,128]{2,1,0:T(8,128)S(1)}, u32[]{:S(2)}, u32[]{:S(2)}) collective-permute-start(f32[64,8,128]{2,1,0:T(8,128)S(1)} %all_to_all.11.back_ref), channel_id=1, source_target_pairs={{0,64},{64,0},{1,65},{65,1},{2,66},{66,2},{3,67},{67,3},{4,68},{68... | collective-permute-start | bytes 786440 | tf_op jit(solution)/shard_map/ppermute | solution.py:321
